TPU v7x, 256 devices: a whole 4x4x8 slice. The times are simulated.
256 devices in a mesh: neuron: 64 (over z, x_hi, y), tm: 4 (over x_lo, core).
Axes of the slice: x: 4 (x_hi: 2, x_lo: 2; x = x_hi * 2 + x_lo), y: 4, z: 8, core: 2. Of those that a mesh axis runs over, the one named last changes fastest.
Arguments:
- data: bfloat16 [8192, 8192], P('neuron', 'tm'), may hold values from 0 to 2
- behaviour: bfloat16 [512, 8192], P('neuron', 'tm'), may hold values from 0 to 2
- motifs: bfloat16 [32, 8192, 128], P('tm', 'neuron'), may hold values from 0 to 2
- behav_motifs: bfloat16 [32, 512, 128], P('tm', 'neuron'), may hold values from 0 to 2
- activations: bfloat16 [128, 8192], P(None, 'tm'), may hold values from 0 to 2
Outputs:
- new_motifs: bfloat16 [32, 8192, 128], P('tm', 'neuron')
- new_behav_motifs: bfloat16 [32, 512, 128], P('tm', 'neuron')
- new_activations: bfloat16 [128, 8192], P(None, 'tm')
All inputs are finite; a program needn't handle non-finite values.
Results may differ from a plain program's by a relative error of at most 0.0034.
Values may be sent and summed in bfloat16 or wider, within the bound.
No kernel may reach another device: no remote copies, remote signals or barrier semaphores. Data moves between devices by JAX's collectives and lax.ppermute only.
A program may use at most 64 MiB of HBM per device.

v0:
```python
import functools
import math

import jax
import jax.numpy as jnp
from jax import lax
from jax.experimental import pallas as pl
from jax.experimental.pallas import tpu as pltpu
from jax.sharding import PartitionSpec as P


behaviour_weight = 2.0
lane = 128
group = 4
deep, wide = 16, 4
patch = 32
f32 = jnp.float32
bf16 = jnp.bfloat16
VMEM = pl.BlockSpec(memory_space=pltpu.VMEM)
HBM = pl.BlockSpec(memory_space=pltpu.HBM)


def crossed(shard, mask):
    return lax.ppermute(shard, "tm", [(i, i ^ mask) for i in range(4)])


def around(shard, by):
    pairs = [(i * wide + y, i * wide + (y + by) % wide) for i in range(deep) for y in range(wide)]
    return lax.ppermute(shard, "neuron", pairs)


def exchanged(blocks):
    groups = [[i * wide + y for i in range(deep)] for y in range(wide)]
    return lax.all_to_all(blocks, "neuron", 0, 0, axis_index_groups=groups, tiled=True)


def place():
    me = lax.axis_index("neuron")
    return me // wide, me % wide


def moved(x, by):
    by = by % x.shape[1]
    return x if by == 0 else pltpu.roll(x, x.shape[1] - by, 1)


def tiles(width, step):
    at = 0
    while at < width:
        size = min(step, width - at)
        yield at, size
        at += size


edge = 32
first_a, last_a, first_d, first_b = 64, 96, 128, 160
pack_rows = 168


def fetched(pairs, sems):
    copies = [pltpu.make_async_copy(source, target, sems.at[i]) for i, (source, target) in enumerate(pairs)]
    for copy in copies:
        copy.start()
    for copy in copies:
        copy.wait()


def pack(v_hbm, active_hbm, data_hbm, behav_hbm, out_ref, v_ref, head_ref, tail_ref, data_ref, behav_ref, sems):
    frames = active_hbm.shape[1]
    fetched(
        [
            (v_hbm, v_ref),
            (active_hbm.at[:, :lane], head_ref),
            (active_hbm.at[:, frames - lane :], tail_ref),
            (data_hbm.at[:, :lane], data_ref),
            (behav_hbm.at[:, :lane], behav_ref),
        ],
        sems,
    )
    out_ref[:first_a] = v_ref[...].reshape(first_a, lane)
    out_ref[first_a:last_a] = head_ref[...].T[:edge]
    out_ref[last_a:first_d] = tail_ref[...].T[lane - edge :]
    out_ref[first_d:first_b] = data_ref[...].T[:edge]
    out_ref[first_b:] = behav_ref[...]


def nearest(odd, near_ref, far_ref, rows):
    mine = lax.axis_index("tm")
    return jnp.where(mine % 2 == odd, near_ref[rows, :], far_ref[rows, :])


def shift_activations(near_ref, far_ref, active_hbm, stack_ref, ext_ref, sems):
    motifs, frames = active_hbm.shape
    width = stack_ref.shape[1]
    steps = stack_ref.shape[0] // motifs
    rows = 16

    def fetch(i):
        part = pl.ds(pl.multiple_of(i * rows, rows), rows)
        return pltpu.make_async_copy(active_hbm.at[part], ext_ref.at[part, lane : lane + frames], sems.at[i])

    for i in range(motifs // rows):
        fetch(i).start()
    blank = jnp.zeros((lane - edge, lane), bf16)
    before = nearest(1, near_ref, far_ref, slice(last_a, first_d))
    before = jnp.where(lax.axis_index("tm") > 0, before, jnp.zeros_like(before))
    after = nearest(0, near_ref, far_ref, slice(first_a, last_a))
    ext_ref[:, :lane] = jnp.concatenate([blank, before], axis=0).T
    ext_ref[:, lane + frames :] = jnp.concatenate([after, blank], axis=0).T

    def chunk(i, carry):
        at = pl.multiple_of(i * rows, rows)
        fetch(i).wait()
        block = ext_ref[pl.ds(at, rows), :]
        for a in range(steps):
            by = lane - (group - 1) - group * a
            stack_ref[pl.ds(pl.multiple_of(a * motifs + at, rows), rows), :] = moved(block, by)[:, :width]
        return carry

    lax.fori_loop(0, motifs // rows, chunk, 0)


def by_lag(w_ref, pack_ref):
    lags = w_ref.shape[0]
    steps = lags // group
    rows = [jnp.concatenate([w_ref[group * a + b] for a in range(steps)], axis=1) for b in range(group)]
    few = first_a // steps
    rows.append(jnp.concatenate([pack_ref[few * a : few * (a + 1), :] for a in range(steps)], axis=1))
    return jnp.concatenate(rows, axis=0)


def forward_half(stack_ref, w0_ref, w1_ref, p0_ref, p1_ref, out_ref):
    mine = lax.axis_index("tm")
    span = stack_ref.shape[0] // 4
    left = jnp.concatenate([by_lag(w0_ref, p0_ref), by_lag(w1_ref, p1_ref)], axis=1)
    starts = [pl.multiple_of((mine ^ p) * span, span) for p in (0, 1)]
    for at, size in tiles(out_ref.shape[1], 256):
        cols = slice(at, at + size)
        right = jnp.concatenate([stack_ref[pl.ds(start, span), cols] for start in starts], axis=0)
        out_ref[:, cols] = jnp.dot(left, right, preferred_element_type=f32)


def forward_backward(scale, frames, *refs):
    base_ref, stack_ref, data_ref, behav_ref = refs[:4]
    w_parts, packs = refs[4:8], refs[8:12]
    grad_refs, resid_ref = refs[12:16], refs[16]
    late_ref, v_ref, out_ref, back_ref, few_ref, turn_ref, sum_ref = refs[17:]
    part, neurons, motifs = w_parts[0].shape
    lags = 4 * part
    features = v_ref.shape[0] // lags
    steps = lags // group
    width = frames + lane
    mine = lax.axis_index("tm")
    _, y = place()
    valid = mine < 3
    parts = list(tiles(width, 256))

    def reach(at, size):
        return slice(at, min(at + size + lane, width))

    left = jnp.concatenate([by_lag(w, p) for w, p in zip(w_parts[2:], packs[2:])], axis=1)
    span = stack_ref.shape[0] // 4
    starts = [pl.multiple_of((mine ^ p) * span, span) for p in (2, 3)]
    after = nearest(0, packs[1], packs[3], slice(first_d, first_b))
    after = jnp.concatenate([after, jnp.zeros((lane - edge, lane), bf16)], axis=0).T
    after_few = nearest(0, packs[1], packs[3], slice(first_b, pack_rows))

    def product(at, size):
        cols = slice(at, at + size)
        right = jnp.concatenate([stack_ref[pl.ds(start, span), cols] for start in starts], axis=0)
        out_ref[:, cols] = jnp.dot(left, right, preferred_element_type=f32) + base_ref[:, cols]

    def recon(first, count, at, size):
        total = None
        for b in range(group):
            rows = slice(first + b * count, first + (b + 1) * count)
            term = moved(out_ref[rows, reach(at, size)], group - 1 - b)[:, :size]
            total = term if total is None else total + term
        return scale * total

    def residual(at, size):
        cols = slice(at, at + size)
        past = at >= frames
        own = after if past else data_ref[:, cols]
        own_few = after_few if past else behav_ref[:, cols]
        resid = own.astype(f32) - recon(0, neurons, at, size)
        few = behaviour_weight * (own_few.astype(f32) - recon(group * neurons, features, at, size))
        if past:
            resid, few = jnp.where(valid, resid, 0.0), jnp.where(valid, few, 0.0)
        resid_ref[:neurons, cols] = resid.astype(bf16)
        resid_ref[neurons:, cols] = few.astype(bf16)

    def spread(at, size):
        block = resid_ref[:neurons, reach(at, size)]
        for a in range(steps):
            back_ref[a * neurons : (a + 1) * neurons, at : at + size] = moved(block, group * a)[:, :size]

    for i, (at, size) in enumerate(parts):
        product(at, size)
        if i == 0:
            for p in range(4):
                v_ref[pl.ds(pl.multiple_of((mine ^ p) * first_a, first_a), first_a)] = packs[p][:first_a, :]
                for a in range(part // group):
                    column = pl.multiple_of((mine ^ p) * span + a * neurons, neurons)
                    for b in range(group):
                        turn_ref[b * motifs : (b + 1) * motifs, pl.ds(column, neurons)] = w_parts[p][group * a + b].T
        if i >= 1:
            residual(*parts[i - 1])
        if i >= 2:
            spread(*parts[i - 2])
    residual(*parts[-1])
    spread(*parts[-2])
    spread(*parts[-1])

    few = resid_ref[neurons:, :].astype(f32)
    for l in range(0, lags, 2):
        pair = jnp.concatenate([moved(few, l)[:, :frames], moved(few, l + 1)[:, :frames]], axis=0)
        few_ref[l * features : (l + 2) * features, :] = pair.astype(bf16)
    v_left = v_ref[...].T

    def gradient(at, size):
        total = jnp.dot(v_left, few_ref[:, at : at + size], preferred_element_type=f32)
        for b in range(group):
            term = late_ref[b * motifs : (b + 1) * motifs, reach(at, size)]
            total = total + moved(term, b)[:, :size]
        for i in range(motifs // patch):
            for j in range(size // lane):
                sum_ref[i * (frames // lane) + at // lane + j] = total[
                    patch * i : patch * (i + 1), lane * j : lane * (j + 1)
                ]

    for i, (at, size) in enumerate(parts):
        cols = slice(at, at + size)
        late_ref[:, cols] = jnp.dot(turn_ref[...], back_ref[:, cols], preferred_element_type=f32)
        if i >= 1:
            gradient(*parts[i - 1])
    for r in range(wide):
        peer = (y + r) % wide
        grad_refs[r][...] = sum_ref[pl.ds(peer * deep, deep)].astype(grad_refs[r].dtype)


def motif_gradients(frames, motifs, stack_ref, resid_ref, keep_ref, relay_ref, send_ref, left_ref):
    out_refs = (keep_ref, send_ref.at[0], relay_ref, send_ref.at[1])
    features = keep_ref.shape[1] - 128
    neurons = resid_ref.shape[0] - features
    steps = stack_ref.shape[0] // motifs
    width = frames + lane
    rows = 16
    mask = lax.broadcasted_iota(jnp.int32, (rows, width), 1) < frames

    def chunk(i, carry):
        at = pl.multiple_of(i * rows, rows)
        block = jnp.where(mask, resid_ref[pl.ds(at, rows), :].astype(f32), 0.0)
        for b in range(group):
            shifted = moved(block, b - (group - 1)).astype(bf16)
            left_ref[pl.ds(pl.multiple_of(b * neurons + at, rows), rows), :] = shifted
        return carry

    lax.fori_loop(0, neurons // rows, chunk, 0)
    block = jnp.where(mask[:features], resid_ref[neurons:, :].astype(f32), 0.0)
    left_ref[group * neurons :, :] = jnp.concatenate(
        [moved(block, b - (group - 1)) for b in range(group)], axis=0
    ).astype(bf16)
    mine = lax.axis_index("tm")
    span = steps * motifs // 4
    for p in (3, 1, 2, 0):
        first = pl.multiple_of((mine ^ p) * span, span)
        result = lax.dot_general(
            left_ref[...], stack_ref[pl.ds(first, span), :], (((1,), (1,)), ((), ())), preferred_element_type=f32
        )
        for a in range(span // motifs):
            for b in range(group):
                target = out_refs[p]
                l = group * a + b
                cols = slice(a * motifs, (a + 1) * motifs)
                few = group * neurons + b * features
                target[l, :neurons, :] = result[b * neurons : (b + 1) * neurons, cols].astype(target.dtype)
                target[l, neurons:, :] = result[few : few + features, cols].astype(target.dtype)


def update_motifs(factor, w_ref, v_ref, keep_ref, got_ref, far_ref, w_out_ref, v_out_ref):
    neurons = w_ref.shape[1]
    lags = w_ref.shape[0]

    def one(l, carry):
        common = far_ref[lags].astype(f32) + far_ref[lags + 1].astype(f32)
        total = keep_ref[l] + got_ref[0, l] + (far_ref[l].astype(f32) + common)
        w_out_ref[l] = jnp.maximum(w_ref[l].astype(f32) + factor * total[:neurons], 0.0).astype(bf16)
        v_out_ref[l] = jnp.maximum(v_ref[l].astype(f32) + factor * total[neurons:], 0.0).astype(bf16)
        return carry

    lax.fori_loop(0, lags, one, 0)


def relay_motifs(relay_ref, got_ref, far_ref):
    lags, rows, _ = relay_ref.shape
    for at, size in tiles(rows, 16):
        part = slice(at, at + size)
        total = relay_ref[:, part, :] + got_ref[1, :, part, :]
        mean = jnp.sum(total, axis=0) * (1.0 / lags)
        high = mean.astype(bf16)
        low = (mean - high.astype(f32)).astype(bf16)
        common = high.astype(f32) + low.astype(f32)
        for l in range(lags):
            far_ref[l, part, :] = (total[l] - common).astype(bf16)
        far_ref[lags, part, :] = high
        far_ref[lags + 1, part, :] = low


def sum_around(*refs):
    parts, out_ref = refs[:wide], refs[wide]
    total = parts[0][...]
    for part in parts[1:]:
        total = total + part[...].astype(f32)
    out_ref[...] = total.astype(out_ref.dtype)


def update(factor, active_hbm, parts_ref, relay_ref, got_ref, out_ref, far_ref, own_ref, sem):
    i, y = place()
    rows = pl.ds(pl.multiple_of(y * patch, patch), patch)
    copy = pltpu.make_async_copy(active_hbm.at[rows, pl.ds(pl.multiple_of(i * lane, lane), lane)], own_ref, sem)
    copy.start()
    total = jnp.sum(parts_ref[...].astype(f32), axis=0)
    copy.wait()
    block = jnp.maximum(own_ref[...].astype(f32) + factor * total, 0.0).astype(bf16)
    for j in range(deep):
        out_ref[j] = block
    relay_motifs(relay_ref, got_ref, far_ref)


def join_columns(parts_ref, out_ref):
    for j in range(deep):
        out_ref[:, lane * j : lane * (j + 1)] = parts_ref[j]


def join_rows(*refs):
    parts, out_ref = refs[:wide], refs[wide]
    _, y = place()
    for r in range(wide):
        row = pl.multiple_of((y + wide - r) % wide * patch, patch)
        out_ref[pl.ds(row, patch), :] = parts[r][...]


def call(body, out_shape, scratch, args, flops=0, moves=1 << 20, vmem=8, in_specs=None):
    if in_specs:
        args = [pltpu.with_memory_space_constraint(a, pltpu.HBM) if p is HBM else a for a, p in zip(args, in_specs)]
    return pl.pallas_call(
        body,
        out_shape=out_shape,
        in_specs=in_specs or [VMEM] * len(args),
        out_specs=jax.tree.map(lambda _: VMEM, out_shape),
        scratch_shapes=scratch,
        compiler_params=pltpu.CompilerParams(vmem_limit_bytes=vmem << 20),
        cost_estimate=pl.CostEstimate(flops=flops, bytes_accessed=moves, transcendentals=0),
    )(*args)


def local(data, behaviour, motifs, behav_motifs, activations):
    lags_here, neurons, width = motifs.shape
    features = behaviour.shape[0]
    frames = activations.shape[1]
    lags = lags_here * lax.axis_size("tm")
    all_frames = frames * lax.axis_size("tm")
    all_neurons = neurons * lax.axis_size("neuron")
    all_features = features * lax.axis_size("neuron")
    scale = 1.0 / (lags * width)
    rate_motif = 0.5 * lags * width / math.sqrt(all_frames)
    rate_active = 0.5 * lags * width / math.sqrt(lags * (all_neurons + 4 * all_features))
    shape = jax.ShapeDtypeStruct
    steps = lags // group

    w2 = crossed(motifs, 2)
    p0 = call(
        pack,
        shape((pack_rows, width), bf16),
        [
            pltpu.VMEM(behav_motifs.shape, bf16),
            pltpu.VMEM((width, lane), bf16),
            pltpu.VMEM((width, lane), bf16),
            pltpu.VMEM((neurons, lane), bf16),
            pltpu.VMEM((features, lane), bf16),
            pltpu.SemaphoreType.DMA((5,)),
        ],
        [behav_motifs, activations, data, behaviour],
        in_specs=[HBM] * 4,
    )
    p2 = crossed(p0, 2)
    p1 = crossed(p0, 1)
    w1 = crossed(motifs, 1)
    p3 = crossed(p2, 1)
    stack = call(
        shift_activations,
        shape((steps * width, frames + lane), bf16),
        [pltpu.VMEM((width, frames + 2 * lane), bf16), pltpu.SemaphoreType.DMA((width // 16,))],
        [p1, p3, activations],
        in_specs=[VMEM, VMEM, HBM],
        moves=8 << 20,
        vmem=8,
    )
    w3 = crossed(w2, 1)
    half = call(
        forward_half,
        shape((group * (neurons + features), frames + lane), f32),
        [],
        [stack, motifs, w1, p0, p1],
        flops=lags * (neurons + features) * width * frames,
        moves=8 << 20,
        vmem=8,
    )

    grads_and_more = call(
        functools.partial(forward_backward, scale, frames),
        [shape((deep, patch, lane), f32 if r == 0 else bf16) for r in range(wide)]
        + [shape((neurons + features, frames + lane), bf16)],
        [
            pltpu.VMEM((group * width, frames + lane), f32),
            pltpu.VMEM((lags * features, width), bf16),
            pltpu.VMEM((group * (neurons + features), frames + lane), f32),
            pltpu.VMEM((steps * neurons, frames + lane), bf16),
            pltpu.VMEM((lags * features, frames), bf16),
            pltpu.VMEM((group * width, steps * neurons), bf16),
            pltpu.VMEM((deep * wide, patch, lane), f32),
        ],
        [half, stack, data, behaviour, motifs, w1, w2, w3, p0, p1, p2, p3],
        flops=3 * lags * (neurons + features) * width * frames,
        moves=4 << 20,
        vmem=24,
    )
    grads, resid = grads_and_more[:wide], grads_and_more[wide]
    around_parts = [grads[0]]
    for r in range(1, wide):
        around_parts.append(around(grads[r], r))

    per_lag = (lags_here, neurons + features, width)
    keep, relay, send = call(
        functools.partial(motif_gradients, frames, width),
        [shape(per_lag, f32), shape(per_lag, f32), shape((2,) + per_lag, f32)],
        [pltpu.VMEM((group * (neurons + features), frames + lane), bf16)],
        [stack, resid],
        flops=2 * lags * (neurons + features) * width * frames,
        moves=4 << 20,
        vmem=8,
    )
    got = crossed(send, 1)

    sums = call(sum_around, shape((deep, patch, lane), bf16), [], around_parts)
    blocks, far = call(
        functools.partial(update, rate_active * scale),
        [shape((deep, patch, lane), bf16), shape((lags_here + 2,) + per_lag[1:], bf16)],
        [pltpu.VMEM((patch, lane), bf16), pltpu.SemaphoreType.DMA],
        [activations, exchanged(sums), relay, got],
        in_specs=[HBM, VMEM, VMEM, VMEM],
    )
    far = crossed(far, 2)
    strip = call(join_columns, shape((patch, frames), bf16), [], [exchanged(blocks)])
    rows = [strip]
    for r in range(1, wide):
        rows.append(around(strip, r))
    new_motifs, new_behav = call(
        functools.partial(update_motifs, rate_motif * scale),
        [shape(motifs.shape, bf16), shape(behav_motifs.shape, bf16)],
        [],
        [motifs, behav_motifs, keep, got, far],
        moves=4 << 20,
    )
    new_active = call(join_rows, shape((width, frames), bf16), [], rows)
    return (new_motifs, new_behav, new_active)


def solution(mesh):
    placed = (
        P("neuron", "tm"),
        P("neuron", "tm"),
        P("tm", "neuron", None),
        P("tm", "neuron", None),
        P(None, "tm"),
    )
    return jax.shard_map(
        local,
        mesh=mesh,
        in_specs=placed,
        out_specs=(P("tm", "neuron", None), P("tm", "neuron", None), P(None, "tm")),
        check_vma=False,
    )
```

profile of v0, /device:TPU:2, one launch (start us, length us, event | category | flops | bytes accessed | tf_op | source)
XLA Modules:
  0.0 89.0 jit_solution(8246095106444404803)
XLA Ops:
  0.6 2.3 %collective-permute-start.4 = (bf16[8,128,128]{2,1,0:T(8,128)(2,1)}, bf16[8,128,128]{2,1,0:T(8,128)(2,1)S(1)}, u32[]{:S(2)}, u32[]{:S(2)}) collective-permute-start(bf16[8,128,128]{2,1,0:T(8,128)(2,1)} %w_ref.1), channel_id=1, source_target_pairs={{0,2},{1,3},{2,0},{3,1},{4,6},{5,7},{6,4},{7,5},{8,10},{9,11},{10,... | collective-permute-start | bytes 786440 | tf_op jit(solution)/shard_map/ppermute | solution.py:24
  3.0 6.0 %collective-permute-done.4.refs_6_ = bf16[8,128,128]{2,1,0:T(8,128)(2,1)S(1)} collective-permute-done((bf16[8,128,128]{2,1,0:T(8,128)(2,1)}, bf16[8,128,128]{2,1,0:T(8,128)(2,1)S(1)}, u32[]{:S(2)}, u32[]{:S(2)}) %collective-permute-start.4) | collective-permute-done | bytes 262176 | tf_op jit(solution)/shard_map/ppermute | solution.py:24
  9.0 0.9 %shard_map.76.p0_ref.refs_8_ = bf16[168,128]{1,0:T(8,128)(2,1)S(1)} custom-call(bf16[8,8,128]{2,1,0:T(8,128)(2,1)} %v_ref.1, bf16[128,2048]{1,0:T(8,128)(2,1)} %active_hbm.5, bf16[128,2048]{1,0:T(8,128)(2,1)} %refs_2_.1, bf16[8,2048]{1,0:T(8,128)(2,1)} %refs_3_.1), custom_call_target="tpu_custom_call" | custom-call | bytes 1048576 | tf_op jit(solution)/shard_map/pallas_call | solution.py:347
  10.8 3.2 %collective-permute-done.1.refs_10_ = bf16[168,128]{1,0:T(8,128)(2,1)S(1)} collective-permute-done((bf16[168,128]{1,0:T(8,128)(2,1)S(1)}, bf16[168,128]{1,0:T(8,128)(2,1)S(1)}, u32[]{:S(2)}, u32[]{:S(2)}) %collective-permute-start.1) | collective-permute-done | bytes 43040 | tf_op jit(solution)/shard_map/ppermute | solution.py:24
  14.0 1.2 %collective-permute-done.2.far_ref.refs_11_ = bf16[168,128]{1,0:T(8,128)(2,1)S(1)} collective-permute-done((bf16[168,128]{1,0:T(8,128)(2,1)S(1)}, bf16[168,128]{1,0:T(8,128)(2,1)S(1)}, u32[]{:S(2)}, u32[]{:S(2)}) %collective-permute-start.2) | collective-permute-done | bytes 43040 | tf_op jit(solution)/shard_map/ppermute | solution.py:24
  15.3 2.7 %shard_map.77.stack_ref.refs_1_ = bf16[1024,2176]{1,0:T(8,128)(2,1)S(1)} custom-call(bf16[168,128]{1,0:T(8,128)(2,1)S(1)} %collective-permute-done.near_ref.p1_ref.refs_9_, bf16[168,128]{1,0:T(8,128)(2,1)S(1)} %collective-permute-done.2.far_ref.refs_11_, bf16[128,2048]{1,0:T(8,128)(2,1)} %active_hbm.5), custom_call_target="tpu_custom_call" | custom-call | bytes 8388608 | tf_op jit(solution)/shard_map/pallas_call | solution.py:347
  18.0 1.5 %shard_map.78.refs_0_ = f32[544,2176]{1,0:T(8,128)S(1)} custom-call(bf16[1024,2176]{1,0:T(8,128)(2,1)S(1)} %shard_map.77.stack_ref.refs_1_, bf16[8,128,128]{2,1,0:T(8,128)(2,1)S(1)} %copy-done, bf16[8,128,128]{2,1,0:T(8,128)(2,1)S(1)} %collective-permute-done.3.w1_ref.refs_5_, bf16[168,128]{1,0:T(8,128)(2,1)S(1)} %shard_map.76.p0_ref.refs_8_, ...), custom_call_target="tpu_custom_call" | custom-call | flops 1140850688 | bytes 8388608 | tf_op jit(solution)/shard_map/pallas_call | solution.py:347
  19.5 5.9 %shard_map.79 = (f32[16,32,128]{2,1,0:T(8,128)S(1)}, bf16[16,32,128]{2,1,0:T(8,128)(2,1)S(1)}, bf16[16,32,128]{2,1,0:T(8,128)(2,1)S(1)}, bf16[16,32,128]{2,1,0:T(8,128)(2,1)S(1)}, bf16[136,2176]{1,0:T(8,128)(2,1)S(1)}) custom-call(f32[544,2176]{1,0:T(8,128)S(1)} %shard_map.78.refs_0_, bf16[1024,2176]{1,0:T(8,128)(2,1)S(1)} %shard_map.77.stack_ref.refs_1_, ...), custom_call_target="tpu_custom_call" | custom-call | flops 3422552064 | bytes 4194304 | tf_op jit(solution)/shard_map/pallas_call | solution.py:347
  25.5 3.9 %shard_map.80 = (f32[8,136,128]{2,1,0:T(8,128)S(1)}, f32[8,136,128]{2,1,0:T(8,128)S(1)}, f32[2,8,136,128]{3,2,1,0:T(8,128)S(1)}) custom-call(bf16[1024,2176]{1,0:T(8,128)(2,1)S(1)} %shard_map.77.stack_ref.refs_1_, bf16[136,2176]{1,0:T(8,128)(2,1)S(1)} %get-tuple-element.15.resid_ref), custom_call_target="tpu_custom_call" | custom-call | flops 2281701376 | bytes 4194304 | tf_op jit(solution)/shard_map/pallas_call | solution.py:347
  29.6 1.6 %collective-permute-start.7 = (bf16[16,32,128]{2,1,0:T(8,128)(2,1)S(1)}, bf16[16,32,128]{2,1,0:T(8,128)(2,1)S(1)}, u32[]{:S(2)}, u32[]{:S(2)}) collective-permute-start(bf16[16,32,128]{2,1,0:T(8,128)(2,1)S(1)} %get-tuple-element.19), channel_id=1, source_target_pairs={{0,4},{4,8},{8,12},{12,0},{16,20},{20,24},{24,28},{28,16},{32,36},... | collective-permute-start | bytes 393224 | tf_op jit(solution)/shard_map/ppermute | solution.py:29
  31.2 2.9 %collective-permute-start.8 = (bf16[16,32,128]{2,1,0:T(8,128)(2,1)S(1)}, bf16[16,32,128]{2,1,0:T(8,128)(2,1)S(1)}, u32[]{:S(2)}, u32[]{:S(2)}) collective-permute-start(bf16[16,32,128]{2,1,0:T(8,128)(2,1)S(1)} %get-tuple-element.20), channel_id=1, source_target_pairs={{0,8},{4,12},{8,0},{12,4},{16,24},{20,28},{24,16},{28,20},{32,40},... | collective-permute-start | bytes 393224 | tf_op jit(solution)/shard_map/ppermute | solution.py:29
  34.1 1.3 %collective-permute-start.9 = (bf16[16,32,128]{2,1,0:T(8,128)(2,1)S(1)}, bf16[16,32,128]{2,1,0:T(8,128)(2,1)S(1)}, u32[]{:S(2)}, u32[]{:S(2)}) collective-permute-start(bf16[16,32,128]{2,1,0:T(8,128)(2,1)S(1)} %get-tuple-element.21), channel_id=1, source_target_pairs={{0,12},{4,0},{8,4},{12,8},{16,28},{20,16},{24,20},{28,24},{32,44},... | collective-permute-start | bytes 393224 | tf_op jit(solution)/shard_map/ppermute | solution.py:29
  35.4 1.2 %collective-permute-done.7.refs_1_ = bf16[16,32,128]{2,1,0:T(8,128)(2,1)S(1)} collective-permute-done((bf16[16,32,128]{2,1,0:T(8,128)(2,1)S(1)}, bf16[16,32,128]{2,1,0:T(8,128)(2,1)S(1)}, u32[]{:S(2)}, u32[]{:S(2)}) %collective-permute-start.7) | collective-permute-done | bytes 131104 | tf_op jit(solution)/shard_map/ppermute | solution.py:29
  36.6 4.0 %collective-permute-done.8.refs_2_ = bf16[16,32,128]{2,1,0:T(8,128)(2,1)S(1)} collective-permute-done((bf16[16,32,128]{2,1,0:T(8,128)(2,1)S(1)}, bf16[16,32,128]{2,1,0:T(8,128)(2,1)S(1)}, u32[]{:S(2)}, u32[]{:S(2)}) %collective-permute-start.8) | collective-permute-done | bytes 131104 | tf_op jit(solution)/shard_map/ppermute | solution.py:29
  40.7 21.0 %all_to_all.10.parts_ref = bf16[16,32,128]{2,1,0:T(8,128)(2,1)S(1)} all-to-all(bf16[16,32,128]{2,1,0:T(8,128)(2,1)S(1)} %shard_map.81), channel_id=1, replica_groups={{0,16,32,48,64,80,96,112,128,144,160,176,192,208,224,240},{4,20,36,52,6..., dimensions={0} | all-to-all | bytes 262144 | tf_op jit(solution)/shard_map/all_to_all | solution.py:34
  61.7 1.4 %shard_map.82 = (bf16[16,32,128]{2,1,0:T(8,128)(2,1)}, bf16[10,136,128]{2,1,0:T(8,128)(2,1)S(1)}) custom-call(bf16[128,2048]{1,0:T(8,128)(2,1)} %active_hbm.5, bf16[16,32,128]{2,1,0:T(8,128)(2,1)S(1)} %all_to_all.10.parts_ref, f32[8,136,128]{2,1,0:T(8,128)S(1)} %get-tuple-element.22.relay_ref, f32[2,8,136,128]{3,2,1,0:T(8,128)S(1)} %collective-permute-done.6.got_ref), custom_call_target="tpu_custom_call" | custom-call | bytes 1048576 | tf_op jit(solution)/shard_map/pallas_call | solution.py:347
  63.1 3.7 %all-to-all-start.1 = ((bf16[16,32,128]{2,1,0:T(8,128)(2,1)}), bf16[16,32,128]{2,1,0:T(8,128)(2,1)S(1)}, u32[]{:S(2)}, u32[]{:S(2)}) async-start(bf16[16,32,128]{2,1,0:T(8,128)(2,1)} %get-tuple-element.26), calls=%async_computation.1 | async-start | bytes 262144 | tf_op jit(solution)/shard_map/all_to_all | solution.py:34
  66.9 1.5 %collective-permute-start.10 = (bf16[10,136,128]{2,1,0:T(8,128)(2,1)S(1)}, bf16[10,136,128]{2,1,0:T(8,128)(2,1)S(1)}, u32[]{:S(2)}, u32[]{:S(2)}) collective-permute-start(bf16[10,136,128]{2,1,0:T(8,128)(2,1)S(1)} %get-tuple-element.23), channel_id=1, source_target_pairs={{0,2},{1,3},{2,0},{3,1},{4,6},{5,7},{6,4},{7,5},{8,10},{9,11},{10,... | collective-permute-start | bytes 1044488 | tf_op jit(solution)/shard_map/ppermute | solution.py:24
  68.4 9.7 %all-to-all-done.1.parts_ref = bf16[16,32,128]{2,1,0:T(8,128)(2,1)S(1)} async-done(((bf16[16,32,128]{2,1,0:T(8,128)(2,1)}), bf16[16,32,128]{2,1,0:T(8,128)(2,1)S(1)}, u32[]{:S(2)}, u32[]{:S(2)}) %all-to-all-start.1) | async-done | bytes 131104 | tf_op jit(solution)/shard_map/all_to_all | solution.py:34
  78.2 2.1 %collective-permute-start.13 = (bf16[32,2048]{1,0:T(8,128)(2,1)S(1)}, bf16[32,2048]{1,0:T(8,128)(2,1)S(1)}, u32[]{:S(2)}, u32[]{:S(2)}) collective-permute-start(bf16[32,2048]{1,0:T(8,128)(2,1)S(1)} %shard_map.84.refs_0_), channel_id=1, source_target_pairs={{0,12},{4,0},{8,4},{12,8},{16,28},{20,16},{24,20},{28,24},{32,44},... | collective-permute-start | bytes 393224 | tf_op jit(solution)/shard_map/ppermute | solution.py:29
  80.3 1.1 %collective-permute-start.12 = (bf16[32,2048]{1,0:T(8,128)(2,1)S(1)}, bf16[32,2048]{1,0:T(8,128)(2,1)S(1)}, u32[]{:S(2)}, u32[]{:S(2)}) collective-permute-start(bf16[32,2048]{1,0:T(8,128)(2,1)S(1)} %shard_map.84.refs_0_), channel_id=1, source_target_pairs={{0,8},{4,12},{8,0},{12,4},{16,24},{20,28},{24,16},{28,20},{32,40},... | collective-permute-start | bytes 393224 | tf_op jit(solution)/shard_map/ppermute | solution.py:29
  82.0 1.0 %shard_map.83 = (bf16[8,128,128]{2,1,0:T(8,128)(2,1)}, bf16[8,8,128]{2,1,0:T(8,128)(2,1)}) custom-call(bf16[8,128,128]{2,1,0:T(8,128)(2,1)S(1)} %copy-done, bf16[8,8,128]{2,1,0:T(8,128)(2,1)S(1)} %copy-done.2, f32[8,136,128]{2,1,0:T(8,128)S(1)} %get-tuple-element.16.keep_ref, f32[2,8,136,128]{3,2,1,0:T(8,128)S(1)} %collective-permute-done.6.got_ref, ...), custom_call_target="tpu_custom_call" | custom-call | bytes 4194304 | tf_op jit(solution)/shard_map/pallas_call | solution.py:347
  83.2 3.6 %collective-permute-done.12.refs_2_ = bf16[32,2048]{1,0:T(8,128)(2,1)S(1)} collective-permute-done((bf16[32,2048]{1,0:T(8,128)(2,1)S(1)}, bf16[32,2048]{1,0:T(8,128)(2,1)S(1)}, u32[]{:S(2)}, u32[]{:S(2)}) %collective-permute-start.12) | collective-permute-done | bytes 131104 | tf_op jit(solution)/shard_map/ppermute | solution.py:29
  86.8 1.3 %collective-permute-done.11.refs_1_ = bf16[32,2048]{1,0:T(8,128)(2,1)S(1)} collective-permute-done((bf16[32,2048]{1,0:T(8,128)(2,1)S(1)}, bf16[32,2048]{1,0:T(8,128)(2,1)S(1)}, u32[]{:S(2)}, u32[]{:S(2)}) %collective-permute-start.11) | collective-permute-done | bytes 131104 | tf_op jit(solution)/shard_map/ppermute | solution.py:29
  (25 shorter events, 2.9 us)
Async XLA Ops:
  0.6 17.4 %copy-start = (bf16[8,128,128]{2,1,0:T(8,128)(2,1)S(1)}, bf16[8,128,128]{2,1,0:T(8,128)(2,1)}, u32[]{:S(2)}) copy-start(bf16[8,128,128]{2,1,0:T(8,128)(2,1)} %w_ref.1) | copy-start | bytes 786436
  0.6 8.3 %collective-permute-start.4 = (bf16[8,128,128]{2,1,0:T(8,128)(2,1)}, bf16[8,128,128]{2,1,0:T(8,128)(2,1)S(1)}, u32[]{:S(2)}, u32[]{:S(2)}) collective-permute-start(bf16[8,128,128]{2,1,0:T(8,128)(2,1)} %w_ref.1), channel_id=1, source_target_pairs={{0,2},{1,3},{2,0},{3,1},{4,6},{5,7},{6,4},{7,5},{8,10},{9,11},{10,... | collective-permute-start | bytes 786440 | tf_op jit(solution)/shard_map/ppermute | solution.py:24
  3.0 15.0 %collective-permute-start.3 = (bf16[8,128,128]{2,1,0:T(8,128)(2,1)}, bf16[8,128,128]{2,1,0:T(8,128)(2,1)S(1)}, u32[]{:S(2)}, u32[]{:S(2)}) collective-permute-start(bf16[8,128,128]{2,1,0:T(8,128)(2,1)} %w_ref.1), channel_id=1, source_target_pairs={{0,1},{1,0},{2,3},{3,2},{4,5},{5,4},{6,7},{7,6},{8,9},{9,8},{10,11... | collective-permute-start | bytes 786440 | tf_op jit(solution)/shard_map/ppermute | solution.py:24
  9.0 10.5 %collective-permute-start.5 = (bf16[8,128,128]{2,1,0:T(8,128)(2,1)S(1)}, bf16[8,128,128]{2,1,0:T(8,128)(2,1)S(1)}, u32[]{:S(2)}, u32[]{:S(2)}) collective-permute-start(bf16[8,128,128]{2,1,0:T(8,128)(2,1)S(1)} %collective-permute-done.4.refs_6_), channel_id=1, source_target_pairs={{0,1},{1,0},{2,3},{3,2},{4,5},{5,4},{6,7},{7,6},{8,9},{9,8},{10,11... | collective-permute-start | bytes 786440 | tf_op jit(solution)/shard_map/ppermute | solution.py:24
  9.9 4.1 %collective-permute-start.1 = (bf16[168,128]{1,0:T(8,128)(2,1)S(1)}, bf16[168,128]{1,0:T(8,128)(2,1)S(1)}, u32[]{:S(2)}, u32[]{:S(2)}) collective-permute-start(bf16[168,128]{1,0:T(8,128)(2,1)S(1)} %shard_map.76.p0_ref.refs_8_), channel_id=1, source_target_pairs={{0,2},{1,3},{2,0},{3,1},{4,6},{5,7},{6,4},{7,5},{8,10},{9,11},{10,... | collective-permute-start | bytes 129032 | tf_op jit(solution)/shard_map/ppermute | solution.py:24
  10.6 3.5 %collective-permute-start = (bf16[168,128]{1,0:T(8,128)(2,1)S(1)}, bf16[168,128]{1,0:T(8,128)(2,1)S(1)}, u32[]{:S(2)}, u32[]{:S(2)}) collective-permute-start(bf16[168,128]{1,0:T(8,128)(2,1)S(1)} %shard_map.76.p0_ref.refs_8_), channel_id=1, source_target_pairs={{0,1},{1,0},{2,3},{3,2},{4,5},{5,4},{6,7},{7,6},{8,9},{9,8},{10,11... | collective-permute-start | bytes 129032 | tf_op jit(solution)/shard_map/ppermute | solution.py:24
  14.0 1.2 %collective-permute-start.2 = (bf16[168,128]{1,0:T(8,128)(2,1)S(1)}, bf16[168,128]{1,0:T(8,128)(2,1)S(1)}, u32[]{:S(2)}, u32[]{:S(2)}) collective-permute-start(bf16[168,128]{1,0:T(8,128)(2,1)S(1)} %collective-permute-done.1.refs_10_), channel_id=1, source_target_pairs={{0,1},{1,0},{2,3},{3,2},{4,5},{5,4},{6,7},{7,6},{8,9},{9,8},{10,11... | collective-permute-start | bytes 129032 | tf_op jit(solution)/shard_map/ppermute | solution.py:24
  18.0 1.5 %copy-start.1 = (bf16[128,2048]{1,0:T(8,128)(2,1)S(1)}, bf16[128,2048]{1,0:T(8,128)(2,1)}, u32[]{:S(2)}) copy-start(bf16[128,2048]{1,0:T(8,128)(2,1)} %refs_2_.1) | copy-start | bytes 1572868
  18.0 1.5 %copy-start.3 = (bf16[8,2048]{1,0:T(8,128)(2,1)S(1)}, bf16[8,2048]{1,0:T(8,128)(2,1)}, u32[]{:S(2)}) copy-start(bf16[8,2048]{1,0:T(8,128)(2,1)} %refs_3_.1) | copy-start | bytes 98308
  25.5 56.5 %copy-start.2 = (bf16[8,8,128]{2,1,0:T(8,128)(2,1)S(1)}, bf16[8,8,128]{2,1,0:T(8,128)(2,1)}, u32[]{:S(2)}) copy-start(bf16[8,8,128]{2,1,0:T(8,128)(2,1)} %v_ref.1) | copy-start | bytes 49156
  29.3 32.4 %collective-permute-start.6 = (f32[2,8,136,128]{3,2,1,0:T(8,128)S(1)}, f32[2,8,136,128]{3,2,1,0:T(8,128)S(1)}, u32[]{:S(2)}, u32[]{:S(2)}) collective-permute-start(f32[2,8,136,128]{3,2,1,0:T(8,128)S(1)} %get-tuple-element.17), channel_id=1, source_target_pairs={{0,1},{1,0},{2,3},{3,2},{4,5},{5,4},{6,7},{7,6},{8,9},{9,8},{10,11... | collective-permute-start | bytes 3342344 | tf_op jit(solution)/shard_map/ppermute | solution.py:24
  29.6 7.0 %collective-permute-start.7 = (bf16[16,32,128]{2,1,0:T(8,128)(2,1)S(1)}, bf16[16,32,128]{2,1,0:T(8,128)(2,1)S(1)}, u32[]{:S(2)}, u32[]{:S(2)}) collective-permute-start(bf16[16,32,128]{2,1,0:T(8,128)(2,1)S(1)} %get-tuple-element.19), channel_id=1, source_target_pairs={{0,4},{4,8},{8,12},{12,0},{16,20},{20,24},{24,28},{28,16},{32,36},... | collective-permute-start | bytes 393224 | tf_op jit(solution)/shard_map/ppermute | solution.py:29
  31.2 9.5 %collective-permute-start.8 = (bf16[16,32,128]{2,1,0:T(8,128)(2,1)S(1)}, bf16[16,32,128]{2,1,0:T(8,128)(2,1)S(1)}, u32[]{:S(2)}, u32[]{:S(2)}) collective-permute-start(bf16[16,32,128]{2,1,0:T(8,128)(2,1)S(1)} %get-tuple-element.20), channel_id=1, source_target_pairs={{0,8},{4,12},{8,0},{12,4},{16,24},{20,28},{24,16},{28,20},{32,40},... | collective-permute-start | bytes 393224 | tf_op jit(solution)/shard_map/ppermute | solution.py:29
  34.1 6.6 %collective-permute-start.9 = (bf16[16,32,128]{2,1,0:T(8,128)(2,1)S(1)}, bf16[16,32,128]{2,1,0:T(8,128)(2,1)S(1)}, u32[]{:S(2)}, u32[]{:S(2)}) collective-permute-start(bf16[16,32,128]{2,1,0:T(8,128)(2,1)S(1)} %get-tuple-element.21), channel_id=1, source_target_pairs={{0,12},{4,0},{8,4},{12,8},{16,28},{20,16},{24,20},{28,24},{32,44},... | collective-permute-start | bytes 393224 | tf_op jit(solution)/shard_map/ppermute | solution.py:29
  63.1 15.0 %all-to-all-start.1 = ((bf16[16,32,128]{2,1,0:T(8,128)(2,1)}), bf16[16,32,128]{2,1,0:T(8,128)(2,1)S(1)}, u32[]{:S(2)}, u32[]{:S(2)}) async-start(bf16[16,32,128]{2,1,0:T(8,128)(2,1)} %get-tuple-element.26), calls=%async_computation.1 | async-start | bytes 262144 | tf_op jit(solution)/shard_map/all_to_all | solution.py:34
  66.9 15.1 %collective-permute-start.10 = (bf16[10,136,128]{2,1,0:T(8,128)(2,1)S(1)}, bf16[10,136,128]{2,1,0:T(8,128)(2,1)S(1)}, u32[]{:S(2)}, u32[]{:S(2)}) collective-permute-start(bf16[10,136,128]{2,1,0:T(8,128)(2,1)S(1)} %get-tuple-element.23), channel_id=1, source_target_pairs={{0,2},{1,3},{2,0},{3,1},{4,6},{5,7},{6,4},{7,5},{8,10},{9,11},{10,... | collective-permute-start | bytes 1044488 | tf_op jit(solution)/shard_map/ppermute | solution.py:24
  78.2 5.0 %collective-permute-start.13 = (bf16[32,2048]{1,0:T(8,128)(2,1)S(1)}, bf16[32,2048]{1,0:T(8,128)(2,1)S(1)}, u32[]{:S(2)}, u32[]{:S(2)}) collective-permute-start(bf16[32,2048]{1,0:T(8,128)(2,1)S(1)} %shard_map.84.refs_0_), channel_id=1, source_target_pairs={{0,12},{4,0},{8,4},{12,8},{16,28},{20,16},{24,20},{28,24},{32,44},... | collective-permute-start | bytes 393224 | tf_op jit(solution)/shard_map/ppermute | solution.py:29
  80.3 6.5 %collective-permute-start.12 = (bf16[32,2048]{1,0:T(8,128)(2,1)S(1)}, bf16[32,2048]{1,0:T(8,128)(2,1)S(1)}, u32[]{:S(2)}, u32[]{:S(2)}) collective-permute-start(bf16[32,2048]{1,0:T(8,128)(2,1)S(1)} %shard_map.84.refs_0_), channel_id=1, source_target_pairs={{0,8},{4,12},{8,0},{12,4},{16,24},{20,28},{24,16},{28,20},{32,40},... | collective-permute-start | bytes 393224 | tf_op jit(solution)/shard_map/ppermute | solution.py:29
  81.4 6.8 %collective-permute-start.11 = (bf16[32,2048]{1,0:T(8,128)(2,1)S(1)}, bf16[32,2048]{1,0:T(8,128)(2,1)S(1)}, u32[]{:S(2)}, u32[]{:S(2)}) collective-permute-start(bf16[32,2048]{1,0:T(8,128)(2,1)S(1)} %shard_map.84.refs_0_), channel_id=1, source_target_pairs={{0,4},{4,8},{8,12},{12,0},{16,20},{20,24},{24,28},{28,16},{32,36},... | collective-permute-start | bytes 393224 | tf_op jit(solution)/shard_map/ppermute | solution.py:29
where the time goes:
time: 89.4 us; the launch traced here: 89 us
  waiting for transfers between devices  30.6 us (34%)
  blocking collectives  21 us (23%)
  starting transfers between devices  18.4 us (21%)
  Pallas kernels  18.2 us (20%)
    all_to_all x1, blocking collectives, exchanged(): lax.all_to_all(blocks, 'neuron', 0, 0, axis_index_groups=groups, tiled=True)  21 us
    pallas_call x10, Pallas kernels, call(): pl.pallas_call(body, out_shape=out_shape, in_specs=in_specs or [VMEM] * l...  18.2 us
    ppermute x8, waiting for transfers between devices, crossed(): return lax.ppermute(shard, 'tm', [(i, i ^ mask) for i in range(4)])  10.5 us
    ppermute x6, waiting for transfers between devices, around(): return lax.ppermute(shard, 'neuron', pairs)  10.4 us
    all_to_all x1, waiting for transfers between devices, exchanged(): lax.all_to_all(blocks, 'neuron', 0, 0, axis_index_groups=groups, tiled=True)  9.71 us
    ppermute x6, starting transfers between devices, around(): return lax.ppermute(shard, 'neuron', pairs)  9.67 us
    ppermute x8, starting transfers between devices, crossed(): return lax.ppermute(shard, 'tm', [(i, i ^ mask) for i in range(4)])  4.99 us
    all_to_all x1, starting transfers between devices, exchanged(): lax.all_to_all(blocks, 'neuron', 0, 0, axis_index_groups=groups, tiled=True)  3.75 us
  transfers between devices with their start and end apart: 15, of which 9 were waited for; matrix products, arithmetic and copies ran while one was open for 0% of the time, Pallas kernels for 7%

commit v1 on v0

--- a/solution.py
+++ b/solution.py
@@ -13,6 +13,7 @@
 lane = 128
 group = 4
 deep, wide = 16, 4
+coarse_step = 1024
 patch = 32
 f32 = jnp.float32
 bf16 = jnp.bfloat16
@@ -129,7 +130,7 @@
     return jnp.concatenate(rows, axis=0)
 
 
-def forward_half(stack_ref, w0_ref, w1_ref, p0_ref, p1_ref, out_ref):
+def forward_half(stack_ref, w0_ref, w1_ref, p0_ref, p1_ref, out_ref, turned_ref):
     mine = lax.axis_index("tm")
     span = stack_ref.shape[0] // 4
     left = jnp.concatenate([by_lag(w0_ref, p0_ref), by_lag(w1_ref, p1_ref)], axis=1)
@@ -138,13 +139,20 @@
         cols = slice(at, at + size)
         right = jnp.concatenate([stack_ref[pl.ds(start, span), cols] for start in starts], axis=0)
         out_ref[:, cols] = jnp.dot(left, right, preferred_element_type=f32)
+        if at == 0:
+            _, neurons, motifs = w0_ref.shape
+            for p, w_ref in enumerate((w0_ref, w1_ref)):
+                for a in range(span // motifs):
+                    first = p * span + a * neurons
+                    for b in range(group):
+                        turned_ref[b * motifs : (b + 1) * motifs, first : first + neurons] = w_ref[group * a + b].T
 
 
 def forward_backward(scale, frames, *refs):
-    base_ref, stack_ref, data_ref, behav_ref = refs[:4]
-    w_parts, packs = refs[4:8], refs[8:12]
-    grad_refs, resid_ref = refs[12:16], refs[16]
-    late_ref, v_ref, out_ref, back_ref, few_ref, turn_ref, sum_ref = refs[17:]
+    base_ref, turned_ref, stack_ref, data_ref, behav_ref = refs[:5]
+    w_parts, packs = refs[5:9], refs[9:13]
+    grad_refs, resid_ref = refs[13:17], refs[17]
+    late_ref, v_ref, out_ref, back_ref, few_ref, turn_ref, sum_ref = refs[18:]
     part, neurons, motifs = w_parts[0].shape
     lags = 4 * part
     features = v_ref.shape[0] // lags
@@ -195,6 +203,8 @@
         for a in range(steps):
             back_ref[a * neurons : (a + 1) * neurons, at : at + size] = moved(block, group * a)[:, :size]
 
+    done = []
+    coarse = list(tiles(width, coarse_step))
     for i, (at, size) in enumerate(parts):
         product(at, size)
         if i == 0:
@@ -203,14 +213,21 @@
                 for a in range(part // group):
                     column = pl.multiple_of((mine ^ p) * span + a * neurons, neurons)
                     for b in range(group):
-                        turn_ref[b * motifs : (b + 1) * motifs, pl.ds(column, neurons)] = w_parts[p][group * a + b].T
-        if i >= 1:
-            residual(*parts[i - 1])
-        if i >= 2:
-            spread(*parts[i - 2])
-    residual(*parts[-1])
-    spread(*parts[-2])
-    spread(*parts[-1])
+                        if p < 2:
+                            turned = turned_ref[
+                                b * motifs : (b + 1) * motifs, p * span + a * neurons : p * span + (a + 1) * neurons
+                            ]
+                        else:
+                            turned = w_parts[p][group * a + b].T
+                        turn_ref[b * motifs : (b + 1) * motifs, pl.ds(column, neurons)] = turned
+        while len(done) < len(coarse) and (
+            reach(*coarse[len(done)]).stop <= at + size
+        ):
+            residual(*coarse[len(done)])
+            if done:
+                spread(*coarse[len(done) - 1])
+            done.append(at)
+    spread(*coarse[-1])
 
     few = resid_ref[neurons:, :].astype(f32)
     for l in range(0, lags, 2):
@@ -229,11 +246,12 @@
                     patch * i : patch * (i + 1), lane * j : lane * (j + 1)
                 ]
 
-    for i, (at, size) in enumerate(parts):
+    waiting = list(tiles(frames, coarse_step))
+    for at, size in parts:
         cols = slice(at, at + size)
         late_ref[:, cols] = jnp.dot(turn_ref[...], back_ref[:, cols], preferred_element_type=f32)
-        if i >= 1:
-            gradient(*parts[i - 1])
+        while waiting and reach(*waiting[0]).stop <= at + size:
+            gradient(*waiting.pop(0))
     for r in range(wide):
         peer = (y + r) % wide
         grad_refs[r][...] = sum_ref[pl.ds(peer * deep, deep)].astype(grad_refs[r].dtype)
@@ -315,7 +333,7 @@
     out_ref[...] = total.astype(out_ref.dtype)
 
 
-def update(factor, active_hbm, parts_ref, relay_ref, got_ref, out_ref, far_ref, own_ref, sem):
+def update(factor, active_hbm, parts_ref, out_ref, own_ref, sem):
     i, y = place()
     rows = pl.ds(pl.multiple_of(y * patch, patch), patch)
     copy = pltpu.make_async_copy(active_hbm.at[rows, pl.ds(pl.multiple_of(i * lane, lane), lane)], own_ref, sem)
@@ -325,7 +343,6 @@
     block = jnp.maximum(own_ref[...].astype(f32) + factor * total, 0.0).astype(bf16)
     for j in range(deep):
         out_ref[j] = block
-    relay_motifs(relay_ref, got_ref, far_ref)
 
 
 def join_columns(parts_ref, out_ref):
@@ -398,9 +415,9 @@
         vmem=8,
     )
     w3 = crossed(w2, 1)
-    half = call(
+    half, turned = call(
         forward_half,
-        shape((group * (neurons + features), frames + lane), f32),
+        [shape((group * (neurons + features), frames + lane), f32), shape((group * width, steps // 2 * neurons), bf16)],
         [],
         [stack, motifs, w1, p0, p1],
         flops=lags * (neurons + features) * width * frames,
@@ -421,7 +438,7 @@
             pltpu.VMEM((group * width, steps * neurons), bf16),
             pltpu.VMEM((deep * wide, patch, lane), f32),
         ],
-        [half, stack, data, behaviour, motifs, w1, w2, w3, p0, p1, p2, p3],
+        [half, turned, stack, data, behaviour, motifs, w1, w2, w3, p0, p1, p2, p3],
         flops=3 * lags * (neurons + features) * width * frames,
         moves=4 << 20,
         vmem=24,
@@ -444,15 +461,23 @@
     got = crossed(send, 1)
 
     sums = call(sum_around, shape((deep, patch, lane), bf16), [], around_parts)
-    blocks, far = call(
+    blocks = call(
         functools.partial(update, rate_active * scale),
-        [shape((deep, patch, lane), bf16), shape((lags_here + 2,) + per_lag[1:], bf16)],
+        shape((deep, patch, lane), bf16),
         [pltpu.VMEM((patch, lane), bf16), pltpu.SemaphoreType.DMA],
-        [activations, exchanged(sums), relay, got],
-        in_specs=[HBM, VMEM, VMEM, VMEM],
+        [activations, exchanged(sums)],
+        in_specs=[HBM, VMEM],
+    )
+    far = call(
+        relay_motifs,
+        shape((lags_here + 2,) + per_lag[1:], bf16),
+        [],
+        [relay, got],
+        moves=4 << 20,
     )
     far = crossed(far, 2)
-    strip = call(join_columns, shape((patch, frames), bf16), [], [exchanged(blocks)])
+    blocks = exchanged(blocks)
+    strip = call(join_columns, shape((patch, frames), bf16), [], [blocks])
     rows = [strip]
     for r in range(1, wide):
         rows.append(around(strip, r))

time: 89.4 us -> 89.1 us (level)
  Pallas kernels: 18.2 us -> 17.2 us
    pallas_call x10 -> x11, Pallas kernels: 18.2 us -> 17.2 us  [call(): pl.pallas_call(body, out_shape=out_shape, in_specs=in_specs or [VMEM] * l...]
  transfers between devices with their start and end apart: 15 -> 15, of which waited for: 9 -> 9; matrix products, arithmetic and copies ran while one was open for 0% -> 0% of each run, Pallas kernels for 7% -> 9%
where the time goes in v1:
time: 89.1 us; the launch traced here: 88.7 us
  waiting for transfers between devices  31.2 us (35%)
  blocking collectives  21.1 us (24%)
  starting transfers between devices  18.4 us (21%)
  Pallas kernels  17.2 us (19%)
    all_to_all x1, blocking collectives, exchanged(): lax.all_to_all(blocks, 'neuron', 0, 0, axis_index_groups=groups, tiled=True)  21.1 us
    pallas_call x11, Pallas kernels, call(): pl.pallas_call(body, out_shape=out_shape, in_specs=in_specs or [VMEM] * l...  17.2 us
    ppermute x6, waiting for transfers between devices, around(): return lax.ppermute(shard, 'neuron', pairs)  11.2 us
    ppermute x8, waiting for transfers between devices, crossed(): return lax.ppermute(shard, 'tm', [(i, i ^ mask) for i in range(4)])  10.5 us
    ppermute x6, starting transfers between devices, around(): return lax.ppermute(shard, 'neuron', pairs)  9.89 us
    all_to_all x1, waiting for transfers between devices, exchanged(): lax.all_to_all(blocks, 'neuron', 0, 0, axis_index_groups=groups, tiled=True)  9.58 us
    ppermute x8, starting transfers between devices, crossed(): return lax.ppermute(shard, 'tm', [(i, i ^ mask) for i in range(4)])  4.99 us
    all_to_all x1, starting transfers between devices, exchanged(): lax.all_to_all(blocks, 'neuron', 0, 0, axis_index_groups=groups, tiled=True)  3.52 us
  transfers between devices with their start and end apart: 15, of which 9 were waited for; matrix products, arithmetic and copies ran while one was open for 0% of the time, Pallas kernels for 9%

profile of v1, /device:TPU:2, one launch (start us, length us, event | category | flops | bytes accessed | tf_op | source)
XLA Modules:
  0.0 88.7 jit_solution(7834437605311388724)
XLA Ops:
  0.6 2.3 %collective-permute-start.4 = (bf16[8,128,128]{2,1,0:T(8,128)(2,1)}, bf16[8,128,128]{2,1,0:T(8,128)(2,1)S(1)}, u32[]{:S(2)}, u32[]{:S(2)}) collective-permute-start(bf16[8,128,128]{2,1,0:T(8,128)(2,1)} %w_ref.1), channel_id=1, source_target_pairs={{0,2},{1,3},{2,0},{3,1},{4,6},{5,7},{6,4},{7,5},{8,10},{9,11},{10,... | collective-permute-start | bytes 786440 | tf_op jit(solution)/shard_map/ppermute | solution.py:25
  3.0 6.0 %collective-permute-done.4.refs_7_ = bf16[8,128,128]{2,1,0:T(8,128)(2,1)S(1)} collective-permute-done((bf16[8,128,128]{2,1,0:T(8,128)(2,1)}, bf16[8,128,128]{2,1,0:T(8,128)(2,1)S(1)}, u32[]{:S(2)}, u32[]{:S(2)}) %collective-permute-start.4) | collective-permute-done | bytes 262176 | tf_op jit(solution)/shard_map/ppermute | solution.py:25
  10.8 3.2 %collective-permute-done.1.refs_11_ = bf16[168,128]{1,0:T(8,128)(2,1)S(1)} collective-permute-done((bf16[168,128]{1,0:T(8,128)(2,1)S(1)}, bf16[168,128]{1,0:T(8,128)(2,1)S(1)}, u32[]{:S(2)}, u32[]{:S(2)}) %collective-permute-start.1) | collective-permute-done | bytes 43040 | tf_op jit(solution)/shard_map/ppermute | solution.py:25
  14.1 1.2 %collective-permute-done.2.far_ref.refs_12_ = bf16[168,128]{1,0:T(8,128)(2,1)S(1)} collective-permute-done((bf16[168,128]{1,0:T(8,128)(2,1)S(1)}, bf16[168,128]{1,0:T(8,128)(2,1)S(1)}, u32[]{:S(2)}, u32[]{:S(2)}) %collective-permute-start.2) | collective-permute-done | bytes 43040 | tf_op jit(solution)/shard_map/ppermute | solution.py:25
  15.3 2.7 %shard_map.77.stack_ref.refs_2_ = bf16[1024,2176]{1,0:T(8,128)(2,1)S(1)} custom-call(bf16[168,128]{1,0:T(8,128)(2,1)S(1)} %collective-permute-done.near_ref.p1_ref.refs_10_, bf16[168,128]{1,0:T(8,128)(2,1)S(1)} %collective-permute-done.2.far_ref.refs_12_, bf16[128,2048]{1,0:T(8,128)(2,1)} %active_hbm.5), custom_call_target="tpu_custom_call" | custom-call | bytes 8388608 | tf_op jit(solution)/shard_map/pallas_call | solution.py:364
  18.0 1.5 %shard_map.78 = (f32[544,2176]{1,0:T(8,128)S(1)}, bf16[512,512]{1,0:T(8,128)(2,1)S(1)}) custom-call(bf16[1024,2176]{1,0:T(8,128)(2,1)S(1)} %shard_map.77.stack_ref.refs_2_, bf16[8,128,128]{2,1,0:T(8,128)(2,1)S(1)} %copy-done, bf16[8,128,128]{2,1,0:T(8,128)(2,1)S(1)} %collective-permute-done.3.w1_ref.refs_6_, bf16[168,128]{1,0:T(8,128)(2,1)S(1)} %shard_map.76.p0_ref.refs_9_, ...), custom_call_target="tpu_custom_call" | custom-call | flops 1140850688 | bytes 8388608 | tf_op jit(solution)/shard_map/pallas_call | solution.py:364
  19.5 4.8 %shard_map.79 = (f32[16,32,128]{2,1,0:T(8,128)S(1)}, bf16[16,32,128]{2,1,0:T(8,128)(2,1)S(1)}, bf16[16,32,128]{2,1,0:T(8,128)(2,1)S(1)}, bf16[16,32,128]{2,1,0:T(8,128)(2,1)S(1)}, bf16[136,2176]{1,0:T(8,128)(2,1)S(1)}) custom-call(f32[544,2176]{1,0:T(8,128)S(1)} %get-tuple-element.15.refs_0_, bf16[512,512]{1,0:T(8,128)(2,1)S(1)} %get-tuple-element.16.refs_1_, ...), custom_call_target="tpu_custom_call" | custom-call | flops 3422552064 | bytes 4194304 | tf_op jit(solution)/shard_map/pallas_call | solution.py:364
  24.4 3.9 %shard_map.80 = (f32[8,136,128]{2,1,0:T(8,128)S(1)}, f32[8,136,128]{2,1,0:T(8,128)S(1)}, f32[2,8,136,128]{3,2,1,0:T(8,128)}) custom-call(bf16[1024,2176]{1,0:T(8,128)(2,1)S(1)} %shard_map.77.stack_ref.refs_2_, bf16[136,2176]{1,0:T(8,128)(2,1)S(1)} %get-tuple-element.17.resid_ref), custom_call_target="tpu_custom_call" | custom-call | flops 2281701376 | bytes 4194304 | tf_op jit(solution)/shard_map/pallas_call | solution.py:364
  28.5 1.7 %collective-permute-start.8 = (bf16[16,32,128]{2,1,0:T(8,128)(2,1)S(1)}, bf16[16,32,128]{2,1,0:T(8,128)(2,1)S(1)}, u32[]{:S(2)}, u32[]{:S(2)}) collective-permute-start(bf16[16,32,128]{2,1,0:T(8,128)(2,1)S(1)} %get-tuple-element.24), channel_id=1, source_target_pairs={{0,4},{4,8},{8,12},{12,0},{16,20},{20,24},{24,28},{28,16},{32,36},... | collective-permute-start | bytes 393224 | tf_op jit(solution)/shard_map/ppermute | solution.py:30
  30.2 2.9 %collective-permute-start.9 = (bf16[16,32,128]{2,1,0:T(8,128)(2,1)S(1)}, bf16[16,32,128]{2,1,0:T(8,128)(2,1)S(1)}, u32[]{:S(2)}, u32[]{:S(2)}) collective-permute-start(bf16[16,32,128]{2,1,0:T(8,128)(2,1)S(1)} %get-tuple-element.25), channel_id=1, source_target_pairs={{0,8},{4,12},{8,0},{12,4},{16,24},{20,28},{24,16},{28,20},{32,40},... | collective-permute-start | bytes 393224 | tf_op jit(solution)/shard_map/ppermute | solution.py:30
  33.1 1.3 %collective-permute-start.10 = (bf16[16,32,128]{2,1,0:T(8,128)(2,1)S(1)}, bf16[16,32,128]{2,1,0:T(8,128)(2,1)S(1)}, u32[]{:S(2)}, u32[]{:S(2)}) collective-permute-start(bf16[16,32,128]{2,1,0:T(8,128)(2,1)S(1)} %get-tuple-element.26), channel_id=1, source_target_pairs={{0,12},{4,0},{8,4},{12,8},{16,28},{20,16},{24,20},{28,24},{32,44},... | collective-permute-start | bytes 393224 | tf_op jit(solution)/shard_map/ppermute | solution.py:30
  34.4 1.1 %collective-permute-done.8.refs_1_ = bf16[16,32,128]{2,1,0:T(8,128)(2,1)S(1)} collective-permute-done((bf16[16,32,128]{2,1,0:T(8,128)(2,1)S(1)}, bf16[16,32,128]{2,1,0:T(8,128)(2,1)S(1)}, u32[]{:S(2)}, u32[]{:S(2)}) %collective-permute-start.8) | collective-permute-done | bytes 131104 | tf_op jit(solution)/shard_map/ppermute | solution.py:30
  35.5 4.0 %collective-permute-done.9.refs_2_ = bf16[16,32,128]{2,1,0:T(8,128)(2,1)S(1)} collective-permute-done((bf16[16,32,128]{2,1,0:T(8,128)(2,1)S(1)}, bf16[16,32,128]{2,1,0:T(8,128)(2,1)S(1)}, u32[]{:S(2)}, u32[]{:S(2)}) %collective-permute-start.9) | collective-permute-done | bytes 131104 | tf_op jit(solution)/shard_map/ppermute | solution.py:30
  39.6 21.1 %all_to_all.10.parts_ref = bf16[16,32,128]{2,1,0:T(8,128)(2,1)S(1)} all-to-all(bf16[16,32,128]{2,1,0:T(8,128)(2,1)S(1)} %shard_map.83), channel_id=1, replica_groups={{0,16,32,48,64,80,96,112,128,144,160,176,192,208,224,240},{4,20,36,52,6..., dimensions={0} | all-to-all | bytes 262144 | tf_op jit(solution)/shard_map/all_to_all | solution.py:35
  60.6 1.4 %shard_map.84 = bf16[16,32,128]{2,1,0:T(8,128)(2,1)} custom-call(bf16[128,2048]{1,0:T(8,128)(2,1)} %active_hbm.5, bf16[16,32,128]{2,1,0:T(8,128)(2,1)S(1)} %all_to_all.10.parts_ref), custom_call_target="tpu_custom_call" | custom-call | bytes 1048576 | tf_op jit(solution)/shard_map/pallas_call | solution.py:364
  62.0 3.5 %all-to-all-start.1 = ((bf16[16,32,128]{2,1,0:T(8,128)(2,1)}), bf16[16,32,128]{2,1,0:T(8,128)(2,1)S(1)}, u32[]{:S(2)}, u32[]{:S(2)}) async-start(bf16[16,32,128]{2,1,0:T(8,128)(2,1)} %shard_map.84), calls=%async_computation.1 | async-start | bytes 262144 | tf_op jit(solution)/shard_map/all_to_all | solution.py:35
  65.7 1.5 %collective-permute-start.7 = (bf16[10,136,128]{2,1,0:T(8,128)(2,1)S(1)}, bf16[10,136,128]{2,1,0:T(8,128)(2,1)S(1)}, u32[]{:S(2)}, u32[]{:S(2)}) collective-permute-start(bf16[10,136,128]{2,1,0:T(8,128)(2,1)S(1)} %shard_map.81), channel_id=1, source_target_pairs={{0,2},{1,3},{2,0},{3,1},{4,6},{5,7},{6,4},{7,5},{8,10},{9,11},{10,... | collective-permute-start | bytes 1044488 | tf_op jit(solution)/shard_map/ppermute | solution.py:25
  67.2 9.6 %all-to-all-done.1.parts_ref = bf16[16,32,128]{2,1,0:T(8,128)(2,1)S(1)} async-done(((bf16[16,32,128]{2,1,0:T(8,128)(2,1)}), bf16[16,32,128]{2,1,0:T(8,128)(2,1)S(1)}, u32[]{:S(2)}, u32[]{:S(2)}) %all-to-all-start.1) | async-done | bytes 131104 | tf_op jit(solution)/shard_map/all_to_all | solution.py:35
  76.8 2.2 %collective-permute-start.13 = (bf16[32,2048]{1,0:T(8,128)(2,1)S(1)}, bf16[32,2048]{1,0:T(8,128)(2,1)S(1)}, u32[]{:S(2)}, u32[]{:S(2)}) collective-permute-start(bf16[32,2048]{1,0:T(8,128)(2,1)S(1)} %shard_map.85.refs_0_), channel_id=1, source_target_pairs={{0,12},{4,0},{8,4},{12,8},{16,28},{20,16},{24,20},{28,24},{32,44},... | collective-permute-start | bytes 393224 | tf_op jit(solution)/shard_map/ppermute | solution.py:30
  79.0 1.1 %collective-permute-start.12 = (bf16[32,2048]{1,0:T(8,128)(2,1)S(1)}, bf16[32,2048]{1,0:T(8,128)(2,1)S(1)}, u32[]{:S(2)}, u32[]{:S(2)}) collective-permute-start(bf16[32,2048]{1,0:T(8,128)(2,1)S(1)} %shard_map.85.refs_0_), channel_id=1, source_target_pairs={{0,8},{4,12},{8,0},{12,4},{16,24},{20,28},{24,16},{28,20},{32,40},... | collective-permute-start | bytes 393224 | tf_op jit(solution)/shard_map/ppermute | solution.py:30
  80.8 1.1 %collective-permute-done.13.refs_3_ = bf16[32,2048]{1,0:T(8,128)(2,1)S(1)} collective-permute-done((bf16[32,2048]{1,0:T(8,128)(2,1)S(1)}, bf16[32,2048]{1,0:T(8,128)(2,1)S(1)}, u32[]{:S(2)}, u32[]{:S(2)}) %collective-permute-start.13) | collective-permute-done | bytes 131104 | tf_op jit(solution)/shard_map/ppermute | solution.py:30
  81.9 3.7 %collective-permute-done.12.refs_2_ = bf16[32,2048]{1,0:T(8,128)(2,1)S(1)} collective-permute-done((bf16[32,2048]{1,0:T(8,128)(2,1)S(1)}, bf16[32,2048]{1,0:T(8,128)(2,1)S(1)}, u32[]{:S(2)}, u32[]{:S(2)}) %collective-permute-start.12) | collective-permute-done | bytes 131104 | tf_op jit(solution)/shard_map/ppermute | solution.py:30
  85.5 1.3 %collective-permute-done.11.refs_1_ = bf16[32,2048]{1,0:T(8,128)(2,1)S(1)} collective-permute-done((bf16[32,2048]{1,0:T(8,128)(2,1)S(1)}, bf16[32,2048]{1,0:T(8,128)(2,1)S(1)}, u32[]{:S(2)}, u32[]{:S(2)}) %collective-permute-start.11) | collective-permute-done | bytes 131104 | tf_op jit(solution)/shard_map/ppermute | solution.py:30
  87.7 1.0 %shard_map.82 = (bf16[8,128,128]{2,1,0:T(8,128)(2,1)}, bf16[8,8,128]{2,1,0:T(8,128)(2,1)}) custom-call(bf16[8,128,128]{2,1,0:T(8,128)(2,1)S(1)} %copy-done, bf16[8,8,128]{2,1,0:T(8,128)(2,1)S(1)} %copy-done.2, f32[8,136,128]{2,1,0:T(8,128)S(1)} %get-tuple-element.18.keep_ref, f32[2,8,136,128]{3,2,1,0:T(8,128)S(1)} %collective-permute-done.6.got_ref, ...), custom_call_target="tpu_custom_call" | custom-call | bytes 4194304 | tf_op jit(solution)/shard_map/pallas_call | solution.py:364
  (26 shorter events, 3.8 us)
Async XLA Ops:
  0.6 17.4 %copy-start = (bf16[8,128,128]{2,1,0:T(8,128)(2,1)S(1)}, bf16[8,128,128]{2,1,0:T(8,128)(2,1)}, u32[]{:S(2)}) copy-start(bf16[8,128,128]{2,1,0:T(8,128)(2,1)} %w_ref.1) | copy-start | bytes 786436
  0.6 8.3 %collective-permute-start.4 = (bf16[8,128,128]{2,1,0:T(8,128)(2,1)}, bf16[8,128,128]{2,1,0:T(8,128)(2,1)S(1)}, u32[]{:S(2)}, u32[]{:S(2)}) collective-permute-start(bf16[8,128,128]{2,1,0:T(8,128)(2,1)} %w_ref.1), channel_id=1, source_target_pairs={{0,2},{1,3},{2,0},{3,1},{4,6},{5,7},{6,4},{7,5},{8,10},{9,11},{10,... | collective-permute-start | bytes 786440 | tf_op jit(solution)/shard_map/ppermute | solution.py:25
  3.0 15.0 %collective-permute-start.3 = (bf16[8,128,128]{2,1,0:T(8,128)(2,1)}, bf16[8,128,128]{2,1,0:T(8,128)(2,1)S(1)}, u32[]{:S(2)}, u32[]{:S(2)}) collective-permute-start(bf16[8,128,128]{2,1,0:T(8,128)(2,1)} %w_ref.1), channel_id=1, source_target_pairs={{0,1},{1,0},{2,3},{3,2},{4,5},{5,4},{6,7},{7,6},{8,9},{9,8},{10,11... | collective-permute-start | bytes 786440 | tf_op jit(solution)/shard_map/ppermute | solution.py:25
  9.0 10.5 %collective-permute-start.5 = (bf16[8,128,128]{2,1,0:T(8,128)(2,1)S(1)}, bf16[8,128,128]{2,1,0:T(8,128)(2,1)S(1)}, u32[]{:S(2)}, u32[]{:S(2)}) collective-permute-start(bf16[8,128,128]{2,1,0:T(8,128)(2,1)S(1)} %collective-permute-done.4.refs_7_), channel_id=1, source_target_pairs={{0,1},{1,0},{2,3},{3,2},{4,5},{5,4},{6,7},{7,6},{8,9},{9,8},{10,11... | collective-permute-start | bytes 786440 | tf_op jit(solution)/shard_map/ppermute | solution.py:25
  9.9 9.6 %copy-start.1 = (bf16[128,2048]{1,0:T(8,128)(2,1)S(1)}, bf16[128,2048]{1,0:T(8,128)(2,1)}, u32[]{:S(2)}) copy-start(bf16[128,2048]{1,0:T(8,128)(2,1)} %refs_3_.1) | copy-start | bytes 1572868
  9.9 9.6 %copy-start.3 = (bf16[8,2048]{1,0:T(8,128)(2,1)S(1)}, bf16[8,2048]{1,0:T(8,128)(2,1)}, u32[]{:S(2)}) copy-start(bf16[8,2048]{1,0:T(8,128)(2,1)} %refs_4_.1) | copy-start | bytes 98308
  9.9 4.1 %collective-permute-start.1 = (bf16[168,128]{1,0:T(8,128)(2,1)S(1)}, bf16[168,128]{1,0:T(8,128)(2,1)S(1)}, u32[]{:S(2)}, u32[]{:S(2)}) collective-permute-start(bf16[168,128]{1,0:T(8,128)(2,1)S(1)} %shard_map.76.p0_ref.refs_9_), channel_id=1, source_target_pairs={{0,2},{1,3},{2,0},{3,1},{4,6},{5,7},{6,4},{7,5},{8,10},{9,11},{10,... | collective-permute-start | bytes 129032 | tf_op jit(solution)/shard_map/ppermute | solution.py:25
  10.6 3.5 %collective-permute-start = (bf16[168,128]{1,0:T(8,128)(2,1)S(1)}, bf16[168,128]{1,0:T(8,128)(2,1)S(1)}, u32[]{:S(2)}, u32[]{:S(2)}) collective-permute-start(bf16[168,128]{1,0:T(8,128)(2,1)S(1)} %shard_map.76.p0_ref.refs_9_), channel_id=1, source_target_pairs={{0,1},{1,0},{2,3},{3,2},{4,5},{5,4},{6,7},{7,6},{8,9},{9,8},{10,11... | collective-permute-start | bytes 129032 | tf_op jit(solution)/shard_map/ppermute | solution.py:25
  14.1 1.2 %collective-permute-start.2 = (bf16[168,128]{1,0:T(8,128)(2,1)S(1)}, bf16[168,128]{1,0:T(8,128)(2,1)S(1)}, u32[]{:S(2)}, u32[]{:S(2)}) collective-permute-start(bf16[168,128]{1,0:T(8,128)(2,1)S(1)} %collective-permute-done.1.refs_11_), channel_id=1, source_target_pairs={{0,1},{1,0},{2,3},{3,2},{4,5},{5,4},{6,7},{7,6},{8,9},{9,8},{10,11... | collective-permute-start | bytes 129032 | tf_op jit(solution)/shard_map/ppermute | solution.py:25
  28.2 59.5 %copy-start.2 = (bf16[8,8,128]{2,1,0:T(8,128)(2,1)S(1)}, bf16[8,8,128]{2,1,0:T(8,128)(2,1)}, u32[]{:S(2)}) copy-start(bf16[8,8,128]{2,1,0:T(8,128)(2,1)} %v_ref.1) | copy-start | bytes 49156
  28.2 37.3 %collective-permute-start.6 = (f32[2,8,136,128]{3,2,1,0:T(8,128)}, f32[2,8,136,128]{3,2,1,0:T(8,128)S(1)}, u32[]{:S(2)}, u32[]{:S(2)}) collective-permute-start(f32[2,8,136,128]{3,2,1,0:T(8,128)} %get-tuple-element.19), channel_id=1, source_target_pairs={{0,1},{1,0},{2,3},{3,2},{4,5},{5,4},{6,7},{7,6},{8,9},{9,8},{10,11... | collective-permute-start | bytes 3342344 | tf_op jit(solution)/shard_map/ppermute | solution.py:25
  28.5 7.0 %collective-permute-start.8 = (bf16[16,32,128]{2,1,0:T(8,128)(2,1)S(1)}, bf16[16,32,128]{2,1,0:T(8,128)(2,1)S(1)}, u32[]{:S(2)}, u32[]{:S(2)}) collective-permute-start(bf16[16,32,128]{2,1,0:T(8,128)(2,1)S(1)} %get-tuple-element.24), channel_id=1, source_target_pairs={{0,4},{4,8},{8,12},{12,0},{16,20},{20,24},{24,28},{28,16},{32,36},... | collective-permute-start | bytes 393224 | tf_op jit(solution)/shard_map/ppermute | solution.py:30
  30.2 9.3 %collective-permute-start.9 = (bf16[16,32,128]{2,1,0:T(8,128)(2,1)S(1)}, bf16[16,32,128]{2,1,0:T(8,128)(2,1)S(1)}, u32[]{:S(2)}, u32[]{:S(2)}) collective-permute-start(bf16[16,32,128]{2,1,0:T(8,128)(2,1)S(1)} %get-tuple-element.25), channel_id=1, source_target_pairs={{0,8},{4,12},{8,0},{12,4},{16,24},{20,28},{24,16},{28,20},{32,40},... | collective-permute-start | bytes 393224 | tf_op jit(solution)/shard_map/ppermute | solution.py:30
  33.1 6.4 %collective-permute-start.10 = (bf16[16,32,128]{2,1,0:T(8,128)(2,1)S(1)}, bf16[16,32,128]{2,1,0:T(8,128)(2,1)S(1)}, u32[]{:S(2)}, u32[]{:S(2)}) collective-permute-start(bf16[16,32,128]{2,1,0:T(8,128)(2,1)S(1)} %get-tuple-element.26), channel_id=1, source_target_pairs={{0,12},{4,0},{8,4},{12,8},{16,28},{20,16},{24,20},{28,24},{32,44},... | collective-permute-start | bytes 393224 | tf_op jit(solution)/shard_map/ppermute | solution.py:30
  62.0 14.8 %all-to-all-start.1 = ((bf16[16,32,128]{2,1,0:T(8,128)(2,1)}), bf16[16,32,128]{2,1,0:T(8,128)(2,1)S(1)}, u32[]{:S(2)}, u32[]{:S(2)}) async-start(bf16[16,32,128]{2,1,0:T(8,128)(2,1)} %shard_map.84), calls=%async_computation.1 | async-start | bytes 262144 | tf_op jit(solution)/shard_map/all_to_all | solution.py:35
  65.7 22.0 %collective-permute-start.7 = (bf16[10,136,128]{2,1,0:T(8,128)(2,1)S(1)}, bf16[10,136,128]{2,1,0:T(8,128)(2,1)S(1)}, u32[]{:S(2)}, u32[]{:S(2)}) collective-permute-start(bf16[10,136,128]{2,1,0:T(8,128)(2,1)S(1)} %shard_map.81), channel_id=1, source_target_pairs={{0,2},{1,3},{2,0},{3,1},{4,6},{5,7},{6,4},{7,5},{8,10},{9,11},{10,... | collective-permute-start | bytes 1044488 | tf_op jit(solution)/shard_map/ppermute | solution.py:25
  76.8 5.0 %collective-permute-start.13 = (bf16[32,2048]{1,0:T(8,128)(2,1)S(1)}, bf16[32,2048]{1,0:T(8,128)(2,1)S(1)}, u32[]{:S(2)}, u32[]{:S(2)}) collective-permute-start(bf16[32,2048]{1,0:T(8,128)(2,1)S(1)} %shard_map.85.refs_0_), channel_id=1, source_target_pairs={{0,12},{4,0},{8,4},{12,8},{16,28},{20,16},{24,20},{28,24},{32,44},... | collective-permute-start | bytes 393224 | tf_op jit(solution)/shard_map/ppermute | solution.py:30
  79.0 6.5 %collective-permute-start.12 = (bf16[32,2048]{1,0:T(8,128)(2,1)S(1)}, bf16[32,2048]{1,0:T(8,128)(2,1)S(1)}, u32[]{:S(2)}, u32[]{:S(2)}) collective-permute-start(bf16[32,2048]{1,0:T(8,128)(2,1)S(1)} %shard_map.85.refs_0_), channel_id=1, source_target_pairs={{0,8},{4,12},{8,0},{12,4},{16,24},{20,28},{24,16},{28,20},{32,40},... | collective-permute-start | bytes 393224 | tf_op jit(solution)/shard_map/ppermute | solution.py:30
  80.1 6.8 %collective-permute-start.11 = (bf16[32,2048]{1,0:T(8,128)(2,1)S(1)}, bf16[32,2048]{1,0:T(8,128)(2,1)S(1)}, u32[]{:S(2)}, u32[]{:S(2)}) collective-permute-start(bf16[32,2048]{1,0:T(8,128)(2,1)S(1)} %shard_map.85.refs_0_), channel_id=1, source_target_pairs={{0,4},{4,8},{8,12},{12,0},{16,20},{20,24},{24,28},{28,16},{32,36},... | collective-permute-start | bytes 393224 | tf_op jit(solution)/shard_map/ppermute | solution.py:30

commit v2 on v1

--- a/solution.py
+++ b/solution.py
@@ -66,21 +66,20 @@
         copy.wait()
 
 
-def pack(v_hbm, active_hbm, data_hbm, behav_hbm, out_ref, v_ref, head_ref, tail_ref, data_ref, behav_ref, sems):
+def pack(v_hbm, active_hbm, data_hbm, behav_hbm, out_ref, active_ref, v_ref, data_ref, behav_ref, sems):
     frames = active_hbm.shape[1]
     fetched(
         [
+            (active_hbm, active_ref),
             (v_hbm, v_ref),
-            (active_hbm.at[:, :lane], head_ref),
-            (active_hbm.at[:, frames - lane :], tail_ref),
             (data_hbm.at[:, :lane], data_ref),
             (behav_hbm.at[:, :lane], behav_ref),
         ],
         sems,
     )
     out_ref[:first_a] = v_ref[...].reshape(first_a, lane)
-    out_ref[first_a:last_a] = head_ref[...].T[:edge]
-    out_ref[last_a:first_d] = tail_ref[...].T[lane - edge :]
+    out_ref[first_a:last_a] = active_ref[:, :lane].T[:edge]
+    out_ref[last_a:first_d] = active_ref[:, frames - lane :].T[lane - edge :]
     out_ref[first_d:first_b] = data_ref[...].T[:edge]
     out_ref[first_b:] = behav_ref[...]
 
@@ -90,28 +89,21 @@
     return jnp.where(mine % 2 == odd, near_ref[rows, :], far_ref[rows, :])
 
 
-def shift_activations(near_ref, far_ref, active_hbm, stack_ref, ext_ref, sems):
-    motifs, frames = active_hbm.shape
+def shift_activations(near_ref, far_ref, active_ref, stack_ref, ext_ref):
+    motifs, frames = active_ref.shape
     width = stack_ref.shape[1]
     steps = stack_ref.shape[0] // motifs
     rows = 16
-
-    def fetch(i):
-        part = pl.ds(pl.multiple_of(i * rows, rows), rows)
-        return pltpu.make_async_copy(active_hbm.at[part], ext_ref.at[part, lane : lane + frames], sems.at[i])
-
-    for i in range(motifs // rows):
-        fetch(i).start()
     blank = jnp.zeros((lane - edge, lane), bf16)
     before = nearest(1, near_ref, far_ref, slice(last_a, first_d))
     before = jnp.where(lax.axis_index("tm") > 0, before, jnp.zeros_like(before))
     after = nearest(0, near_ref, far_ref, slice(first_a, last_a))
     ext_ref[:, :lane] = jnp.concatenate([blank, before], axis=0).T
+    ext_ref[:, lane : lane + frames] = active_ref[...]
     ext_ref[:, lane + frames :] = jnp.concatenate([after, blank], axis=0).T
 
     def chunk(i, carry):
         at = pl.multiple_of(i * rows, rows)
-        fetch(i).wait()
         block = ext_ref[pl.ds(at, rows), :]
         for a in range(steps):
             by = lane - (group - 1) - group * a
@@ -333,14 +325,11 @@
     out_ref[...] = total.astype(out_ref.dtype)
 
 
-def update(factor, active_hbm, parts_ref, out_ref, own_ref, sem):
+def update(factor, active_ref, parts_ref, out_ref):
     i, y = place()
-    rows = pl.ds(pl.multiple_of(y * patch, patch), patch)
-    copy = pltpu.make_async_copy(active_hbm.at[rows, pl.ds(pl.multiple_of(i * lane, lane), lane)], own_ref, sem)
-    copy.start()
+    own = active_ref[pl.ds(pl.multiple_of(y * patch, patch), patch), pl.ds(pl.multiple_of(i * lane, lane), lane)]
     total = jnp.sum(parts_ref[...].astype(f32), axis=0)
-    copy.wait()
-    block = jnp.maximum(own_ref[...].astype(f32) + factor * total, 0.0).astype(bf16)
+    block = jnp.maximum(own.astype(f32) + factor * total, 0.0).astype(bf16)
     for j in range(deep):
         out_ref[j] = block
 
@@ -387,16 +376,14 @@
     steps = lags // group
 
     w2 = crossed(motifs, 2)
-    p0 = call(
+    p0, active = call(
         pack,
-        shape((pack_rows, width), bf16),
+        [shape((pack_rows, width), bf16), shape(activations.shape, bf16)],
         [
             pltpu.VMEM(behav_motifs.shape, bf16),
-            pltpu.VMEM((width, lane), bf16),
-            pltpu.VMEM((width, lane), bf16),
             pltpu.VMEM((neurons, lane), bf16),
             pltpu.VMEM((features, lane), bf16),
-            pltpu.SemaphoreType.DMA((5,)),
+            pltpu.SemaphoreType.DMA((4,)),
         ],
         [behav_motifs, activations, data, behaviour],
         in_specs=[HBM] * 4,
@@ -408,9 +395,8 @@
     stack = call(
         shift_activations,
         shape((steps * width, frames + lane), bf16),
-        [pltpu.VMEM((width, frames + 2 * lane), bf16), pltpu.SemaphoreType.DMA((width // 16,))],
-        [p1, p3, activations],
-        in_specs=[VMEM, VMEM, HBM],
+        [pltpu.VMEM((width, frames + 2 * lane), bf16)],
+        [p1, p3, active],
         moves=8 << 20,
         vmem=8,
     )
@@ -464,9 +450,8 @@
     blocks = call(
         functools.partial(update, rate_active * scale),
         shape((deep, patch, lane), bf16),
-        [pltpu.VMEM((patch, lane), bf16), pltpu.SemaphoreType.DMA],
-        [activations, exchanged(sums)],
-        in_specs=[HBM, VMEM],
+        [],
+        [active, exchanged(sums)],
     )
     far = call(
         relay_motifs,

time: 89.1 us -> 87.5 us (0.982)
  Pallas kernels: 17.2 us -> 15.9 us
    pallas_call x11, Pallas kernels: 17.2 us -> 15.9 us  [call(): pl.pallas_call(body, out_shape=out_shape, in_specs=in_specs or [VMEM] * l...]
  transfers between devices with their start and end apart: 15 -> 15, of which waited for: 9 -> 9; matrix products, arithmetic and copies ran while one was open for 0% -> 0% of each run, Pallas kernels for 9% -> 7%
where the time goes in v2:
time: 87.5 us; the launch traced here: 87.3 us
  waiting for transfers between devices  31.2 us (36%)
  blocking collectives  21 us (24%)
  starting transfers between devices  18.4 us (21%)
  Pallas kernels  15.9 us (18%)
    all_to_all x1, blocking collectives, exchanged(): lax.all_to_all(blocks, 'neuron', 0, 0, axis_index_groups=groups, tiled=True)  21 us
    pallas_call x11, Pallas kernels, call(): pl.pallas_call(body, out_shape=out_shape, in_specs=in_specs or [VMEM] * l...  15.9 us
    ppermute x6, waiting for transfers between devices, around(): return lax.ppermute(shard, 'neuron', pairs)  11.2 us
    ppermute x8, waiting for transfers between devices, crossed(): return lax.ppermute(shard, 'tm', [(i, i ^ mask) for i in range(4)])  10.5 us
    ppermute x6, starting transfers between devices, around(): return lax.ppermute(shard, 'neuron', pairs)  9.9 us
    all_to_all x1, waiting for transfers between devices, exchanged(): lax.all_to_all(blocks, 'neuron', 0, 0, axis_index_groups=groups, tiled=True)  9.59 us
    ppermute x8, starting transfers between devices, crossed(): return lax.ppermute(shard, 'tm', [(i, i ^ mask) for i in range(4)])  5 us
    all_to_all x1, starting transfers between devices, exchanged(): lax.all_to_all(blocks, 'neuron', 0, 0, axis_index_groups=groups, tiled=True)  3.51 us
  transfers between devices with their start and end apart: 15, of which 9 were waited for; matrix products, arithmetic and copies ran while one was open for 0% of the time, Pallas kernels for 7%

profile of v2, /device:TPU:2, one launch (start us, length us, event | category | flops | bytes accessed | tf_op | source)
XLA Modules:
  0.0 87.3 jit_solution(16075487300019442386)
XLA Ops:
  0.6 2.3 %collective-permute-start.4 = (bf16[8,128,128]{2,1,0:T(8,128)(2,1)}, bf16[8,128,128]{2,1,0:T(8,128)(2,1)S(1)}, u32[]{:S(2)}, u32[]{:S(2)}) collective-permute-start(bf16[8,128,128]{2,1,0:T(8,128)(2,1)} %w_ref.1), channel_id=1, source_target_pairs={{0,2},{1,3},{2,0},{3,1},{4,6},{5,7},{6,4},{7,5},{8,10},{9,11},{10,... | collective-permute-start | bytes 786440 | tf_op jit(solution)/shard_map/ppermute | solution.py:25
  3.0 6.0 %collective-permute-done.4.refs_7_ = bf16[8,128,128]{2,1,0:T(8,128)(2,1)S(1)} collective-permute-done((bf16[8,128,128]{2,1,0:T(8,128)(2,1)}, bf16[8,128,128]{2,1,0:T(8,128)(2,1)S(1)}, u32[]{:S(2)}, u32[]{:S(2)}) %collective-permute-start.4) | collective-permute-done | bytes 262176 | tf_op jit(solution)/shard_map/ppermute | solution.py:25
  9.0 1.2 %shard_map.76 = (bf16[168,128]{1,0:T(8,128)(2,1)S(1)}, bf16[128,2048]{1,0:T(8,128)(2,1)S(1)}) custom-call(bf16[8,8,128]{2,1,0:T(8,128)(2,1)} %v_ref.1, bf16[128,2048]{1,0:T(8,128)(2,1)} %active_hbm.1, bf16[128,2048]{1,0:T(8,128)(2,1)} %refs_3_.1, bf16[8,2048]{1,0:T(8,128)(2,1)} %refs_4_.1), custom_call_target="tpu_custom_call" | custom-call | bytes 1048576 | tf_op jit(solution)/shard_map/pallas_call | solution.py:353
  11.0 3.2 %collective-permute-done.1.refs_11_ = bf16[168,128]{1,0:T(8,128)(2,1)S(1)} collective-permute-done((bf16[168,128]{1,0:T(8,128)(2,1)S(1)}, bf16[168,128]{1,0:T(8,128)(2,1)S(1)}, u32[]{:S(2)}, u32[]{:S(2)}) %collective-permute-start.1) | collective-permute-done | bytes 43040 | tf_op jit(solution)/shard_map/ppermute | solution.py:25
  14.3 1.2 %collective-permute-done.2.far_ref.refs_12_ = bf16[168,128]{1,0:T(8,128)(2,1)S(1)} collective-permute-done((bf16[168,128]{1,0:T(8,128)(2,1)S(1)}, bf16[168,128]{1,0:T(8,128)(2,1)S(1)}, u32[]{:S(2)}, u32[]{:S(2)}) %collective-permute-start.2) | collective-permute-done | bytes 43040 | tf_op jit(solution)/shard_map/ppermute | solution.py:25
  15.5 1.9 %shard_map.77.stack_ref.refs_2_ = bf16[1024,2176]{1,0:T(8,128)(2,1)S(1)} custom-call(bf16[168,128]{1,0:T(8,128)(2,1)S(1)} %collective-permute-done.near_ref.p1_ref.refs_10_, bf16[168,128]{1,0:T(8,128)(2,1)S(1)} %collective-permute-done.2.far_ref.refs_12_, bf16[128,2048]{1,0:T(8,128)(2,1)S(1)} %get-tuple-element.18.active_ref), custom_call_target="tpu_custom_call" | custom-call | bytes 8388608 | tf_op jit(solution)/shard_map/pallas_call | solution.py:353
  17.4 1.5 %shard_map.78 = (f32[544,2176]{1,0:T(8,128)S(1)}, bf16[512,512]{1,0:T(8,128)(2,1)S(1)}) custom-call(bf16[1024,2176]{1,0:T(8,128)(2,1)S(1)} %shard_map.77.stack_ref.refs_2_, bf16[8,128,128]{2,1,0:T(8,128)(2,1)S(1)} %copy-done, bf16[8,128,128]{2,1,0:T(8,128)(2,1)S(1)} %collective-permute-done.3.w1_ref.refs_6_, ...), custom_call_target="tpu_custom_call" | custom-call | flops 1140850688 | bytes 8388608 | tf_op jit(solution)/shard_map/pallas_call | solution.py:353
  18.9 4.8 %shard_map.79 = (f32[16,32,128]{2,1,0:T(8,128)S(1)}, bf16[16,32,128]{2,1,0:T(8,128)(2,1)S(1)}, bf16[16,32,128]{2,1,0:T(8,128)(2,1)S(1)}, bf16[16,32,128]{2,1,0:T(8,128)(2,1)S(1)}, bf16[136,2176]{1,0:T(8,128)(2,1)S(1)}) custom-call(f32[544,2176]{1,0:T(8,128)S(1)} %get-tuple-element.19.refs_0_, bf16[512,512]{1,0:T(8,128)(2,1)S(1)} %get-tuple-element.20.refs_1_, ...), custom_call_target="tpu_custom_call" | custom-call | flops 3422552064 | bytes 4194304 | tf_op jit(solution)/shard_map/pallas_call | solution.py:353
  23.7 3.9 %shard_map.80 = (f32[8,136,128]{2,1,0:T(8,128)S(1)}, f32[8,136,128]{2,1,0:T(8,128)S(1)}, f32[2,8,136,128]{3,2,1,0:T(8,128)}) custom-call(bf16[1024,2176]{1,0:T(8,128)(2,1)S(1)} %shard_map.77.stack_ref.refs_2_, bf16[136,2176]{1,0:T(8,128)(2,1)S(1)} %get-tuple-element.21.resid_ref), custom_call_target="tpu_custom_call" | custom-call | flops 2281701376 | bytes 4194304 | tf_op jit(solution)/shard_map/pallas_call | solution.py:353
  27.9 1.7 %collective-permute-start.8 = (bf16[16,32,128]{2,1,0:T(8,128)(2,1)S(1)}, bf16[16,32,128]{2,1,0:T(8,128)(2,1)S(1)}, u32[]{:S(2)}, u32[]{:S(2)}) collective-permute-start(bf16[16,32,128]{2,1,0:T(8,128)(2,1)S(1)} %get-tuple-element.28), channel_id=1, source_target_pairs={{0,4},{4,8},{8,12},{12,0},{16,20},{20,24},{24,28},{28,16},{32,36},... | collective-permute-start | bytes 393224 | tf_op jit(solution)/shard_map/ppermute | solution.py:30
  29.5 2.9 %collective-permute-start.9 = (bf16[16,32,128]{2,1,0:T(8,128)(2,1)S(1)}, bf16[16,32,128]{2,1,0:T(8,128)(2,1)S(1)}, u32[]{:S(2)}, u32[]{:S(2)}) collective-permute-start(bf16[16,32,128]{2,1,0:T(8,128)(2,1)S(1)} %get-tuple-element.29), channel_id=1, source_target_pairs={{0,8},{4,12},{8,0},{12,4},{16,24},{20,28},{24,16},{28,20},{32,40},... | collective-permute-start | bytes 393224 | tf_op jit(solution)/shard_map/ppermute | solution.py:30
  32.5 1.3 %collective-permute-start.10 = (bf16[16,32,128]{2,1,0:T(8,128)(2,1)S(1)}, bf16[16,32,128]{2,1,0:T(8,128)(2,1)S(1)}, u32[]{:S(2)}, u32[]{:S(2)}) collective-permute-start(bf16[16,32,128]{2,1,0:T(8,128)(2,1)S(1)} %get-tuple-element.30), channel_id=1, source_target_pairs={{0,12},{4,0},{8,4},{12,8},{16,28},{20,16},{24,20},{28,24},{32,44},... | collective-permute-start | bytes 393224 | tf_op jit(solution)/shard_map/ppermute | solution.py:30
  33.8 1.1 %collective-permute-done.8.refs_1_ = bf16[16,32,128]{2,1,0:T(8,128)(2,1)S(1)} collective-permute-done((bf16[16,32,128]{2,1,0:T(8,128)(2,1)S(1)}, bf16[16,32,128]{2,1,0:T(8,128)(2,1)S(1)}, u32[]{:S(2)}, u32[]{:S(2)}) %collective-permute-start.8) | collective-permute-done | bytes 131104 | tf_op jit(solution)/shard_map/ppermute | solution.py:30
  34.9 4.0 %collective-permute-done.9.refs_2_ = bf16[16,32,128]{2,1,0:T(8,128)(2,1)S(1)} collective-permute-done((bf16[16,32,128]{2,1,0:T(8,128)(2,1)S(1)}, bf16[16,32,128]{2,1,0:T(8,128)(2,1)S(1)}, u32[]{:S(2)}, u32[]{:S(2)}) %collective-permute-start.9) | collective-permute-done | bytes 131104 | tf_op jit(solution)/shard_map/ppermute | solution.py:30
  38.9 21.0 %all_to_all.10.parts_ref = bf16[16,32,128]{2,1,0:T(8,128)(2,1)S(1)} all-to-all(bf16[16,32,128]{2,1,0:T(8,128)(2,1)S(1)} %shard_map.83), channel_id=1, replica_groups={{0,16,32,48,64,80,96,112,128,144,160,176,192,208,224,240},{4,20,36,52,6..., dimensions={0} | all-to-all | bytes 262144 | tf_op jit(solution)/shard_map/all_to_all | solution.py:35
  60.7 3.5 %all-to-all-start.1 = ((bf16[16,32,128]{2,1,0:T(8,128)(2,1)}), bf16[16,32,128]{2,1,0:T(8,128)(2,1)S(1)}, u32[]{:S(2)}, u32[]{:S(2)}) async-start(bf16[16,32,128]{2,1,0:T(8,128)(2,1)} %shard_map.84), calls=%async_computation.1 | async-start | bytes 262144 | tf_op jit(solution)/shard_map/all_to_all | solution.py:35
  64.3 1.5 %collective-permute-start.7 = (bf16[10,136,128]{2,1,0:T(8,128)(2,1)S(1)}, bf16[10,136,128]{2,1,0:T(8,128)(2,1)S(1)}, u32[]{:S(2)}, u32[]{:S(2)}) collective-permute-start(bf16[10,136,128]{2,1,0:T(8,128)(2,1)S(1)} %shard_map.81), channel_id=1, source_target_pairs={{0,2},{1,3},{2,0},{3,1},{4,6},{5,7},{6,4},{7,5},{8,10},{9,11},{10,... | collective-permute-start | bytes 1044488 | tf_op jit(solution)/shard_map/ppermute | solution.py:25
  65.8 9.6 %all-to-all-done.1.parts_ref = bf16[16,32,128]{2,1,0:T(8,128)(2,1)S(1)} async-done(((bf16[16,32,128]{2,1,0:T(8,128)(2,1)}), bf16[16,32,128]{2,1,0:T(8,128)(2,1)S(1)}, u32[]{:S(2)}, u32[]{:S(2)}) %all-to-all-start.1) | async-done | bytes 131104 | tf_op jit(solution)/shard_map/all_to_all | solution.py:35
  75.5 2.2 %collective-permute-start.13 = (bf16[32,2048]{1,0:T(8,128)(2,1)S(1)}, bf16[32,2048]{1,0:T(8,128)(2,1)S(1)}, u32[]{:S(2)}, u32[]{:S(2)}) collective-permute-start(bf16[32,2048]{1,0:T(8,128)(2,1)S(1)} %shard_map.85.refs_0_), channel_id=1, source_target_pairs={{0,12},{4,0},{8,4},{12,8},{16,28},{20,16},{24,20},{28,24},{32,44},... | collective-permute-start | bytes 393224 | tf_op jit(solution)/shard_map/ppermute | solution.py:30
  77.6 1.1 %collective-permute-start.12 = (bf16[32,2048]{1,0:T(8,128)(2,1)S(1)}, bf16[32,2048]{1,0:T(8,128)(2,1)S(1)}, u32[]{:S(2)}, u32[]{:S(2)}) collective-permute-start(bf16[32,2048]{1,0:T(8,128)(2,1)S(1)} %shard_map.85.refs_0_), channel_id=1, source_target_pairs={{0,8},{4,12},{8,0},{12,4},{16,24},{20,28},{24,16},{28,20},{32,40},... | collective-permute-start | bytes 393224 | tf_op jit(solution)/shard_map/ppermute | solution.py:30
  79.4 1.1 %collective-permute-done.13.refs_3_ = bf16[32,2048]{1,0:T(8,128)(2,1)S(1)} collective-permute-done((bf16[32,2048]{1,0:T(8,128)(2,1)S(1)}, bf16[32,2048]{1,0:T(8,128)(2,1)S(1)}, u32[]{:S(2)}, u32[]{:S(2)}) %collective-permute-start.13) | collective-permute-done | bytes 131104 | tf_op jit(solution)/shard_map/ppermute | solution.py:30
  80.5 3.7 %collective-permute-done.12.refs_2_ = bf16[32,2048]{1,0:T(8,128)(2,1)S(1)} collective-permute-done((bf16[32,2048]{1,0:T(8,128)(2,1)S(1)}, bf16[32,2048]{1,0:T(8,128)(2,1)S(1)}, u32[]{:S(2)}, u32[]{:S(2)}) %collective-permute-start.12) | collective-permute-done | bytes 131104 | tf_op jit(solution)/shard_map/ppermute | solution.py:30
  84.1 1.3 %collective-permute-done.11.refs_1_ = bf16[32,2048]{1,0:T(8,128)(2,1)S(1)} collective-permute-done((bf16[32,2048]{1,0:T(8,128)(2,1)S(1)}, bf16[32,2048]{1,0:T(8,128)(2,1)S(1)}, u32[]{:S(2)}, u32[]{:S(2)}) %collective-permute-start.11) | collective-permute-done | bytes 131104 | tf_op jit(solution)/shard_map/ppermute | solution.py:30
  86.3 1.0 %shard_map.82 = (bf16[8,128,128]{2,1,0:T(8,128)(2,1)}, bf16[8,8,128]{2,1,0:T(8,128)(2,1)}) custom-call(bf16[8,128,128]{2,1,0:T(8,128)(2,1)S(1)} %copy-done, bf16[8,8,128]{2,1,0:T(8,128)(2,1)S(1)} %copy-done.2, f32[8,136,128]{2,1,0:T(8,128)S(1)} %get-tuple-element.22.keep_ref, f32[2,8,136,128]{3,2,1,0:T(8,128)S(1)} %collective-permute-done.6.got_ref, ...), custom_call_target="tpu_custom_call" | custom-call | bytes 4194304 | tf_op jit(solution)/shard_map/pallas_call | solution.py:353
  (26 shorter events, 3.5 us)
Async XLA Ops:
  0.6 16.7 %copy-start = (bf16[8,128,128]{2,1,0:T(8,128)(2,1)S(1)}, bf16[8,128,128]{2,1,0:T(8,128)(2,1)}, u32[]{:S(2)}) copy-start(bf16[8,128,128]{2,1,0:T(8,128)(2,1)} %w_ref.1) | copy-start | bytes 786436
  0.6 8.3 %collective-permute-start.4 = (bf16[8,128,128]{2,1,0:T(8,128)(2,1)}, bf16[8,128,128]{2,1,0:T(8,128)(2,1)S(1)}, u32[]{:S(2)}, u32[]{:S(2)}) collective-permute-start(bf16[8,128,128]{2,1,0:T(8,128)(2,1)} %w_ref.1), channel_id=1, source_target_pairs={{0,2},{1,3},{2,0},{3,1},{4,6},{5,7},{6,4},{7,5},{8,10},{9,11},{10,... | collective-permute-start | bytes 786440 | tf_op jit(solution)/shard_map/ppermute | solution.py:25
  3.0 14.4 %collective-permute-start.3 = (bf16[8,128,128]{2,1,0:T(8,128)(2,1)}, bf16[8,128,128]{2,1,0:T(8,128)(2,1)S(1)}, u32[]{:S(2)}, u32[]{:S(2)}) collective-permute-start(bf16[8,128,128]{2,1,0:T(8,128)(2,1)} %w_ref.1), channel_id=1, source_target_pairs={{0,1},{1,0},{2,3},{3,2},{4,5},{5,4},{6,7},{7,6},{8,9},{9,8},{10,11... | collective-permute-start | bytes 786440 | tf_op jit(solution)/shard_map/ppermute | solution.py:25
  9.0 9.9 %collective-permute-start.5 = (bf16[8,128,128]{2,1,0:T(8,128)(2,1)S(1)}, bf16[8,128,128]{2,1,0:T(8,128)(2,1)S(1)}, u32[]{:S(2)}, u32[]{:S(2)}) collective-permute-start(bf16[8,128,128]{2,1,0:T(8,128)(2,1)S(1)} %collective-permute-done.4.refs_7_), channel_id=1, source_target_pairs={{0,1},{1,0},{2,3},{3,2},{4,5},{5,4},{6,7},{7,6},{8,9},{9,8},{10,11... | collective-permute-start | bytes 786440 | tf_op jit(solution)/shard_map/ppermute | solution.py:25
  10.2 4.1 %collective-permute-start.1 = (bf16[168,128]{1,0:T(8,128)(2,1)S(1)}, bf16[168,128]{1,0:T(8,128)(2,1)S(1)}, u32[]{:S(2)}, u32[]{:S(2)}) collective-permute-start(bf16[168,128]{1,0:T(8,128)(2,1)S(1)} %get-tuple-element.17.p0_ref.refs_9_), channel_id=1, source_target_pairs={{0,2},{1,3},{2,0},{3,1},{4,6},{5,7},{6,4},{7,5},{8,10},{9,11},{10,... | collective-permute-start | bytes 129032 | tf_op jit(solution)/shard_map/ppermute | solution.py:25
  10.8 3.5 %collective-permute-start = (bf16[168,128]{1,0:T(8,128)(2,1)S(1)}, bf16[168,128]{1,0:T(8,128)(2,1)S(1)}, u32[]{:S(2)}, u32[]{:S(2)}) collective-permute-start(bf16[168,128]{1,0:T(8,128)(2,1)S(1)} %get-tuple-element.17.p0_ref.refs_9_), channel_id=1, source_target_pairs={{0,1},{1,0},{2,3},{3,2},{4,5},{5,4},{6,7},{7,6},{8,9},{9,8},{10,11... | collective-permute-start | bytes 129032 | tf_op jit(solution)/shard_map/ppermute | solution.py:25
  14.3 1.2 %collective-permute-start.2 = (bf16[168,128]{1,0:T(8,128)(2,1)S(1)}, bf16[168,128]{1,0:T(8,128)(2,1)S(1)}, u32[]{:S(2)}, u32[]{:S(2)}) collective-permute-start(bf16[168,128]{1,0:T(8,128)(2,1)S(1)} %collective-permute-done.1.refs_11_), channel_id=1, source_target_pairs={{0,1},{1,0},{2,3},{3,2},{4,5},{5,4},{6,7},{7,6},{8,9},{9,8},{10,11... | collective-permute-start | bytes 129032 | tf_op jit(solution)/shard_map/ppermute | solution.py:25
  15.5 3.4 %copy-start.1 = (bf16[128,2048]{1,0:T(8,128)(2,1)S(1)}, bf16[128,2048]{1,0:T(8,128)(2,1)}, u32[]{:S(2)}) copy-start(bf16[128,2048]{1,0:T(8,128)(2,1)} %refs_3_.1) | copy-start | bytes 1572868
  15.5 3.4 %copy-start.3 = (bf16[8,2048]{1,0:T(8,128)(2,1)S(1)}, bf16[8,2048]{1,0:T(8,128)(2,1)}, u32[]{:S(2)}) copy-start(bf16[8,2048]{1,0:T(8,128)(2,1)} %refs_4_.1) | copy-start | bytes 98308
  27.6 58.8 %copy-start.2 = (bf16[8,8,128]{2,1,0:T(8,128)(2,1)S(1)}, bf16[8,8,128]{2,1,0:T(8,128)(2,1)}, u32[]{:S(2)}) copy-start(bf16[8,8,128]{2,1,0:T(8,128)(2,1)} %v_ref.1) | copy-start | bytes 49156
  27.6 36.6 %collective-permute-start.6 = (f32[2,8,136,128]{3,2,1,0:T(8,128)}, f32[2,8,136,128]{3,2,1,0:T(8,128)S(1)}, u32[]{:S(2)}, u32[]{:S(2)}) collective-permute-start(f32[2,8,136,128]{3,2,1,0:T(8,128)} %get-tuple-element.23), channel_id=1, source_target_pairs={{0,1},{1,0},{2,3},{3,2},{4,5},{5,4},{6,7},{7,6},{8,9},{9,8},{10,11... | collective-permute-start | bytes 3342344 | tf_op jit(solution)/shard_map/ppermute | solution.py:25
  27.9 7.0 %collective-permute-start.8 = (bf16[16,32,128]{2,1,0:T(8,128)(2,1)S(1)}, bf16[16,32,128]{2,1,0:T(8,128)(2,1)S(1)}, u32[]{:S(2)}, u32[]{:S(2)}) collective-permute-start(bf16[16,32,128]{2,1,0:T(8,128)(2,1)S(1)} %get-tuple-element.28), channel_id=1, source_target_pairs={{0,4},{4,8},{8,12},{12,0},{16,20},{20,24},{24,28},{28,16},{32,36},... | collective-permute-start | bytes 393224 | tf_op jit(solution)/shard_map/ppermute | solution.py:30
  29.5 9.3 %collective-permute-start.9 = (bf16[16,32,128]{2,1,0:T(8,128)(2,1)S(1)}, bf16[16,32,128]{2,1,0:T(8,128)(2,1)S(1)}, u32[]{:S(2)}, u32[]{:S(2)}) collective-permute-start(bf16[16,32,128]{2,1,0:T(8,128)(2,1)S(1)} %get-tuple-element.29), channel_id=1, source_target_pairs={{0,8},{4,12},{8,0},{12,4},{16,24},{20,28},{24,16},{28,20},{32,40},... | collective-permute-start | bytes 393224 | tf_op jit(solution)/shard_map/ppermute | solution.py:30
  32.5 6.4 %collective-permute-start.10 = (bf16[16,32,128]{2,1,0:T(8,128)(2,1)S(1)}, bf16[16,32,128]{2,1,0:T(8,128)(2,1)S(1)}, u32[]{:S(2)}, u32[]{:S(2)}) collective-permute-start(bf16[16,32,128]{2,1,0:T(8,128)(2,1)S(1)} %get-tuple-element.30), channel_id=1, source_target_pairs={{0,12},{4,0},{8,4},{12,8},{16,28},{20,16},{24,20},{28,24},{32,44},... | collective-permute-start | bytes 393224 | tf_op jit(solution)/shard_map/ppermute | solution.py:30
  60.7 14.8 %all-to-all-start.1 = ((bf16[16,32,128]{2,1,0:T(8,128)(2,1)}), bf16[16,32,128]{2,1,0:T(8,128)(2,1)S(1)}, u32[]{:S(2)}, u32[]{:S(2)}) async-start(bf16[16,32,128]{2,1,0:T(8,128)(2,1)} %shard_map.84), calls=%async_computation.1 | async-start | bytes 262144 | tf_op jit(solution)/shard_map/all_to_all | solution.py:35
  64.3 22.0 %collective-permute-start.7 = (bf16[10,136,128]{2,1,0:T(8,128)(2,1)S(1)}, bf16[10,136,128]{2,1,0:T(8,128)(2,1)S(1)}, u32[]{:S(2)}, u32[]{:S(2)}) collective-permute-start(bf16[10,136,128]{2,1,0:T(8,128)(2,1)S(1)} %shard_map.81), channel_id=1, source_target_pairs={{0,2},{1,3},{2,0},{3,1},{4,6},{5,7},{6,4},{7,5},{8,10},{9,11},{10,... | collective-permute-start | bytes 1044488 | tf_op jit(solution)/shard_map/ppermute | solution.py:25
  75.5 5.0 %collective-permute-start.13 = (bf16[32,2048]{1,0:T(8,128)(2,1)S(1)}, bf16[32,2048]{1,0:T(8,128)(2,1)S(1)}, u32[]{:S(2)}, u32[]{:S(2)}) collective-permute-start(bf16[32,2048]{1,0:T(8,128)(2,1)S(1)} %shard_map.85.refs_0_), channel_id=1, source_target_pairs={{0,12},{4,0},{8,4},{12,8},{16,28},{20,16},{24,20},{28,24},{32,44},... | collective-permute-start | bytes 393224 | tf_op jit(solution)/shard_map/ppermute | solution.py:30
  77.6 6.5 %collective-permute-start.12 = (bf16[32,2048]{1,0:T(8,128)(2,1)S(1)}, bf16[32,2048]{1,0:T(8,128)(2,1)S(1)}, u32[]{:S(2)}, u32[]{:S(2)}) collective-permute-start(bf16[32,2048]{1,0:T(8,128)(2,1)S(1)} %shard_map.85.refs_0_), channel_id=1, source_target_pairs={{0,8},{4,12},{8,0},{12,4},{16,24},{20,28},{24,16},{28,20},{32,40},... | collective-permute-start | bytes 393224 | tf_op jit(solution)/shard_map/ppermute | solution.py:30
  78.7 6.7 %collective-permute-start.11 = (bf16[32,2048]{1,0:T(8,128)(2,1)S(1)}, bf16[32,2048]{1,0:T(8,128)(2,1)S(1)}, u32[]{:S(2)}, u32[]{:S(2)}) collective-permute-start(bf16[32,2048]{1,0:T(8,128)(2,1)S(1)} %shard_map.85.refs_0_), channel_id=1, source_target_pairs={{0,4},{4,8},{8,12},{12,0},{16,20},{20,24},{24,28},{28,16},{32,36},... | collective-permute-start | bytes 393224 | tf_op jit(solution)/shard_map/ppermute | solution.py:30

commit v3 on v2

--- a/solution.py
+++ b/solution.py
@@ -89,28 +89,18 @@
     return jnp.where(mine % 2 == odd, near_ref[rows, :], far_ref[rows, :])
 
 
-def shift_activations(near_ref, far_ref, active_ref, stack_ref, ext_ref):
+def shifted_edges(near_ref, far_ref, active_ref, edge_ref):
     motifs, frames = active_ref.shape
-    width = stack_ref.shape[1]
-    steps = stack_ref.shape[0] // motifs
-    rows = 16
     blank = jnp.zeros((lane - edge, lane), bf16)
     before = nearest(1, near_ref, far_ref, slice(last_a, first_d))
     before = jnp.where(lax.axis_index("tm") > 0, before, jnp.zeros_like(before))
     after = nearest(0, near_ref, far_ref, slice(first_a, last_a))
-    ext_ref[:, :lane] = jnp.concatenate([blank, before], axis=0).T
-    ext_ref[:, lane : lane + frames] = active_ref[...]
-    ext_ref[:, lane + frames :] = jnp.concatenate([after, blank], axis=0).T
-
-    def chunk(i, carry):
-        at = pl.multiple_of(i * rows, rows)
-        block = ext_ref[pl.ds(at, rows), :]
-        for a in range(steps):
-            by = lane - (group - 1) - group * a
-            stack_ref[pl.ds(pl.multiple_of(a * motifs + at, rows), rows), :] = moved(block, by)[:, :width]
-        return carry
-
-    lax.fori_loop(0, motifs // rows, chunk, 0)
+    first = jnp.concatenate([jnp.concatenate([blank, before], axis=0).T, active_ref[:, :lane]], axis=1)
+    last = jnp.concatenate([active_ref[:, frames - lane :], jnp.concatenate([after, blank], axis=0).T], axis=1)
+    for a in range(edge_ref.shape[0] // motifs):
+        by = lane - (group - 1) - group * a
+        edge_ref[a * motifs : (a + 1) * motifs, :lane] = moved(first, by)[:, :lane]
+        edge_ref[a * motifs : (a + 1) * motifs, lane:] = moved(last, by)[:, :lane]
 
 
 def by_lag(w_ref, pack_ref):
@@ -122,16 +112,29 @@
     return jnp.concatenate(rows, axis=0)
 
 
-def forward_half(stack_ref, w0_ref, w1_ref, p0_ref, p1_ref, out_ref, turned_ref):
+def forward_half(active_ref, w0_ref, w1_ref, p0_ref, p1_ref, stack_ref, out_ref, turned_ref):
+    motifs, frames = active_ref.shape
+    rows = 16
+
+    def chunk(i, carry):
+        at = pl.multiple_of(i * rows, rows)
+        block = active_ref[pl.ds(at, rows), :]
+        for a in range(stack_ref.shape[0] // motifs):
+            shifted = moved(block, -(group - 1) - group * a)
+            stack_ref[pl.ds(pl.multiple_of(a * motifs + at, rows), rows), :] = shifted
+        return carry
+
+    lax.fori_loop(0, motifs // rows, chunk, 0)
+
     mine = lax.axis_index("tm")
     span = stack_ref.shape[0] // 4
     left = jnp.concatenate([by_lag(w0_ref, p0_ref), by_lag(w1_ref, p1_ref)], axis=1)
     starts = [pl.multiple_of((mine ^ p) * span, span) for p in (0, 1)]
-    for at, size in tiles(out_ref.shape[1], 256):
+    for at, size in list(tiles(frames, 256))[1:]:
         cols = slice(at, at + size)
         right = jnp.concatenate([stack_ref[pl.ds(start, span), cols] for start in starts], axis=0)
         out_ref[:, cols] = jnp.dot(left, right, preferred_element_type=f32)
-        if at == 0:
+        if at == 256:
             _, neurons, motifs = w0_ref.shape
             for p, w_ref in enumerate((w0_ref, w1_ref)):
                 for a in range(span // motifs):
@@ -141,10 +144,10 @@
 
 
 def forward_backward(scale, frames, *refs):
-    base_ref, turned_ref, stack_ref, data_ref, behav_ref = refs[:5]
-    w_parts, packs = refs[5:9], refs[9:13]
-    grad_refs, resid_ref = refs[13:17], refs[17]
-    late_ref, v_ref, out_ref, back_ref, few_ref, turn_ref, sum_ref = refs[18:]
+    base_ref, turned_ref, stack_ref, active_ref, data_ref, behav_ref = refs[:6]
+    w_parts, packs = refs[6:10], refs[10:14]
+    grad_refs, resid_ref, edge_ref = refs[14:18], refs[18], refs[19]
+    late_ref, v_ref, out_ref, back_ref, few_ref, turn_ref, sum_ref = refs[20:]
     part, neurons, motifs = w_parts[0].shape
     lags = 4 * part
     features = v_ref.shape[0] // lags
@@ -158,17 +161,28 @@
     def reach(at, size):
         return slice(at, min(at + size + lane, width))
 
-    left = jnp.concatenate([by_lag(w, p) for w, p in zip(w_parts[2:], packs[2:])], axis=1)
+    shifted_edges(packs[1], packs[3], active_ref, edge_ref)
+    lefts = [by_lag(w, p) for w, p in zip(w_parts, packs)]
     span = stack_ref.shape[0] // 4
-    starts = [pl.multiple_of((mine ^ p) * span, span) for p in (2, 3)]
+    starts = [pl.multiple_of((mine ^ p) * span, span) for p in range(4)]
     after = nearest(0, packs[1], packs[3], slice(first_d, first_b))
     after = jnp.concatenate([after, jnp.zeros((lane - edge, lane), bf16)], axis=0).T
     after_few = nearest(0, packs[1], packs[3], slice(first_b, pack_rows))
 
+    def shifted(p, at, size):
+        rows = pl.ds(starts[p], span)
+        if at == 0:
+            return jnp.concatenate([edge_ref[rows, :lane], stack_ref[rows, lane:size]], axis=1)
+        return edge_ref[rows, lane:] if at >= frames else stack_ref[rows, at : at + size]
+
     def product(at, size):
         cols = slice(at, at + size)
-        right = jnp.concatenate([stack_ref[pl.ds(start, span), cols] for start in starts], axis=0)
-        out_ref[:, cols] = jnp.dot(left, right, preferred_element_type=f32) + base_ref[:, cols]
+        whole = at == 0 or at >= frames
+        these = range(4) if whole else (2, 3)
+        left = jnp.concatenate([lefts[p] for p in these], axis=1)
+        right = jnp.concatenate([shifted(p, at, size) for p in these], axis=0)
+        part = jnp.dot(left, right, preferred_element_type=f32)
+        out_ref[:, cols] = part if whole else part + base_ref[:, cols]
 
     def recon(first, count, at, size):
         total = None
@@ -249,7 +263,7 @@
         grad_refs[r][...] = sum_ref[pl.ds(peer * deep, deep)].astype(grad_refs[r].dtype)
 
 
-def motif_gradients(frames, motifs, stack_ref, resid_ref, keep_ref, relay_ref, send_ref, left_ref):
+def motif_gradients(frames, motifs, stack_ref, edge_ref, resid_ref, keep_ref, relay_ref, send_ref, left_ref):
     out_refs = (keep_ref, send_ref.at[0], relay_ref, send_ref.at[1])
     features = keep_ref.shape[1] - 128
     neurons = resid_ref.shape[0] - features
@@ -275,9 +289,11 @@
     span = steps * motifs // 4
     for p in (3, 1, 2, 0):
         first = pl.multiple_of((mine ^ p) * span, span)
-        result = lax.dot_general(
-            left_ref[...], stack_ref[pl.ds(first, span), :], (((1,), (1,)), ((), ())), preferred_element_type=f32
+        part = pl.ds(first, span)
+        right = jnp.concatenate(
+            [edge_ref[part, :lane], stack_ref[part, lane:], edge_ref[part, lane:]], axis=1
         )
+        result = lax.dot_general(left_ref[...], right, (((1,), (1,)), ((), ())), preferred_element_type=f32)
         for a in range(span // motifs):
             for b in range(group):
                 target = out_refs[p]
@@ -376,6 +392,7 @@
     steps = lags // group
 
     w2 = crossed(motifs, 2)
+    w1 = crossed(motifs, 1)
     p0, active = call(
         pack,
         [shape((pack_rows, width), bf16), shape(activations.shape, bf16)],
@@ -388,33 +405,28 @@
         [behav_motifs, activations, data, behaviour],
         in_specs=[HBM] * 4,
     )
+    p3 = crossed(p0, 3)
     p2 = crossed(p0, 2)
     p1 = crossed(p0, 1)
-    w1 = crossed(motifs, 1)
-    p3 = crossed(p2, 1)
-    stack = call(
-        shift_activations,
-        shape((steps * width, frames + lane), bf16),
-        [pltpu.VMEM((width, frames + 2 * lane), bf16)],
-        [p1, p3, active],
-        moves=8 << 20,
-        vmem=8,
-    )
     w3 = crossed(w2, 1)
-    half, turned = call(
+    stack, half, turned = call(
         forward_half,
-        [shape((group * (neurons + features), frames + lane), f32), shape((group * width, steps // 2 * neurons), bf16)],
+        [
+            shape((steps * width, frames), bf16),
+            shape((group * (neurons + features), frames + lane), f32),
+            shape((group * width, steps // 2 * neurons), bf16),
+        ],
         [],
-        [stack, motifs, w1, p0, p1],
+        [active, motifs, w1, p0, p1],
         flops=lags * (neurons + features) * width * frames,
         moves=8 << 20,
-        vmem=8,
+        vmem=16,
     )
 
     grads_and_more = call(
         functools.partial(forward_backward, scale, frames),
         [shape((deep, patch, lane), f32 if r == 0 else bf16) for r in range(wide)]
-        + [shape((neurons + features, frames + lane), bf16)],
+        + [shape((neurons + features, frames + lane), bf16), shape((steps * width, 2 * lane), bf16)],
         [
             pltpu.VMEM((group * width, frames + lane), f32),
             pltpu.VMEM((lags * features, width), bf16),
@@ -424,12 +436,12 @@
             pltpu.VMEM((group * width, steps * neurons), bf16),
             pltpu.VMEM((deep * wide, patch, lane), f32),
         ],
-        [half, turned, stack, data, behaviour, motifs, w1, w2, w3, p0, p1, p2, p3],
+        [half, turned, stack, active, data, behaviour, motifs, w1, w2, w3, p0, p1, p2, p3],
         flops=3 * lags * (neurons + features) * width * frames,
         moves=4 << 20,
         vmem=24,
     )
-    grads, resid = grads_and_more[:wide], grads_and_more[wide]
+    grads, resid, edges = grads_and_more[:wide], grads_and_more[wide], grads_and_more[wide + 1]
     around_parts = [grads[0]]
     for r in range(1, wide):
         around_parts.append(around(grads[r], r))
@@ -439,7 +451,7 @@
         functools.partial(motif_gradients, frames, width),
         [shape(per_lag, f32), shape(per_lag, f32), shape((2,) + per_lag, f32)],
         [pltpu.VMEM((group * (neurons + features), frames + lane), bf16)],
-        [stack, resid],
+        [stack, edges, resid],
         flops=2 * lags * (neurons + features) * width * frames,
         moves=4 << 20,
         vmem=8,

time: 87.5 us -> 85.8 us (0.981)
  waiting for transfers between devices: 31.2 us -> 26.8 us
  starting transfers between devices: 18.4 us -> 20 us
  local copies, waits for them, and re-layouts: 0.02 us -> 0.97 us
    ppermute x8, waiting for transfers between devices: 10.5 us -> 6.03 us  [crossed(): return lax.ppermute(shard, 'tm', [(i, i ^ mask) for i in range(4)])]
    ppermute x8, starting transfers between devices: 5 us -> 6.57 us  [crossed(): return lax.ppermute(shard, 'tm', [(i, i ^ mask) for i in range(4)])]
    unnamed x8 -> x10, local copies, waits for them, and re-layouts: 0.02 us -> 0.97 us
    pallas_call x11 -> x10, Pallas kernels: 15.9 us -> 16 us  [call(): pl.pallas_call(body, out_shape=out_shape, in_specs=in_specs or [VMEM] * l...]
  transfers between devices with their start and end apart: 15 -> 15, of which waited for: 9 -> 7; matrix products, arithmetic and copies ran while one was open for 0% -> 0% of each run, Pallas kernels for 7% -> 7%
where the time goes in v3:
time: 85.8 us; the launch traced here: 85.6 us
  waiting for transfers between devices  26.8 us (31%)
  blocking collectives  21.1 us (25%)
  starting transfers between devices  20 us (23%)
  Pallas kernels  16 us (19%)
  local copies, waits for them, and re-layouts  0.97 us (1%)
    all_to_all x1, blocking collectives, exchanged(): lax.all_to_all(blocks, 'neuron', 0, 0, axis_index_groups=groups, tiled=True)  21.1 us
    pallas_call x10, Pallas kernels, call(): pl.pallas_call(body, out_shape=out_shape, in_specs=in_specs or [VMEM] * l...  16 us
    ppermute x6, waiting for transfers between devices, around(): return lax.ppermute(shard, 'neuron', pairs)  11.2 us
    ppermute x6, starting transfers between devices, around(): return lax.ppermute(shard, 'neuron', pairs)  9.89 us
    all_to_all x1, waiting for transfers between devices, exchanged(): lax.all_to_all(blocks, 'neuron', 0, 0, axis_index_groups=groups, tiled=True)  9.59 us
    ppermute x8, starting transfers between devices, crossed(): return lax.ppermute(shard, 'tm', [(i, i ^ mask) for i in range(4)])  6.57 us
    ppermute x8, waiting for transfers between devices, crossed(): return lax.ppermute(shard, 'tm', [(i, i ^ mask) for i in range(4)])  6.03 us
    all_to_all x1, starting transfers between devices, exchanged(): lax.all_to_all(blocks, 'neuron', 0, 0, axis_index_groups=groups, tiled=True)  3.51 us
  transfers between devices with their start and end apart: 15, of which 7 were waited for; matrix products, arithmetic and copies ran while one was open for 0% of the time, Pallas kernels for 7%

profile of v3, /device:TPU:2, one launch (start us, length us, event | category | flops | bytes accessed | tf_op | source)
XLA Modules:
  0.0 85.6 jit_solution(9533980826825436831)
XLA Ops:
  0.7 2.3 %collective-permute-start.2 = (bf16[8,128,128]{2,1,0:T(8,128)(2,1)}, bf16[8,128,128]{2,1,0:T(8,128)(2,1)S(1)}, u32[]{:S(2)}, u32[]{:S(2)}) collective-permute-start(bf16[8,128,128]{2,1,0:T(8,128)(2,1)} %w_ref.1), channel_id=1, source_target_pairs={{0,2},{1,3},{2,0},{3,1},{4,6},{5,7},{6,4},{7,5},{8,10},{9,11},{10,... | collective-permute-start | bytes 786440 | tf_op jit(solution)/shard_map/ppermute | solution.py:25
  3.0 6.0 %collective-permute-done.2.refs_8_ = bf16[8,128,128]{2,1,0:T(8,128)(2,1)S(1)} collective-permute-done((bf16[8,128,128]{2,1,0:T(8,128)(2,1)}, bf16[8,128,128]{2,1,0:T(8,128)(2,1)S(1)}, u32[]{:S(2)}, u32[]{:S(2)}) %collective-permute-start.2) | collective-permute-done | bytes 262176 | tf_op jit(solution)/shard_map/ppermute | solution.py:25
  9.0 1.2 %shard_map.76 = (bf16[168,128]{1,0:T(8,128)(2,1)S(1)}, bf16[128,2048]{1,0:T(8,128)(2,1)S(1)}) custom-call(bf16[8,8,128]{2,1,0:T(8,128)(2,1)} %v_ref.1, bf16[128,2048]{1,0:T(8,128)(2,1)} %active_hbm.1, bf16[128,2048]{1,0:T(8,128)(2,1)} %refs_4_.1, bf16[8,2048]{1,0:T(8,128)(2,1)} %refs_5_.1), custom_call_target="tpu_custom_call" | custom-call | bytes 1048576 | tf_op jit(solution)/shard_map/pallas_call | solution.py:369
  11.0 1.5 %collective-permute-start.4 = (bf16[168,128]{1,0:T(8,128)(2,1)S(1)}, bf16[168,128]{1,0:T(8,128)(2,1)S(1)}, u32[]{:S(2)}, u32[]{:S(2)}) collective-permute-start(bf16[168,128]{1,0:T(8,128)(2,1)S(1)} %get-tuple-element.20.p0_ref.refs_10_), channel_id=1, source_target_pairs={{0,2},{1,3},{2,0},{3,1},{4,6},{5,7},{6,4},{7,5},{8,10},{9,11},{10,... | collective-permute-start | bytes 129032 | tf_op jit(solution)/shard_map/ppermute | solution.py:25
  12.5 0.9 %copy-done.1 = bf16[8,128,128]{2,1,0:T(8,128)(2,1)S(1)} copy-done((bf16[8,128,128]{2,1,0:T(8,128)(2,1)S(1)}, bf16[8,128,128]{2,1,0:T(8,128)(2,1)}, u32[]{:S(2)}) %copy-start.1) | copy-done | bytes 262168
  13.5 2.8 %shard_map.77 = (bf16[1024,2048]{1,0:T(8,128)(2,1)S(1)}, f32[544,2176]{1,0:T(8,128)S(1)}, bf16[512,512]{1,0:T(8,128)(2,1)S(1)}) custom-call(bf16[128,2048]{1,0:T(8,128)(2,1)S(1)} %get-tuple-element.19.active_ref.refs_3_, bf16[8,128,128]{2,1,0:T(8,128)(2,1)S(1)} %copy-done.1, bf16[8,128,128]{2,1,0:T(8,128)(2,1)S(1)} %collective-permute-done.w1_ref.refs_7_, ...), custom_call_target="tpu_custom_call" | custom-call | flops 1140850688 | bytes 8388608 | tf_op jit(solution)/shard_map/pallas_call | solution.py:369
  16.4 5.4 %shard_map.78 = (f32[16,32,128]{2,1,0:T(8,128)S(1)}, bf16[16,32,128]{2,1,0:T(8,128)(2,1)S(1)}, bf16[16,32,128]{2,1,0:T(8,128)(2,1)S(1)}, bf16[16,32,128]{2,1,0:T...) custom-call(f32[544,2176]{1,0:T(8,128)S(1)} %get-tuple-element.22.refs_0_, ...), custom_call_target="tpu_custom_call" | custom-call | flops 3422552064 | bytes 4194304 | tf_op jit(solution)/shard_map/pallas_call | solution.py:369
  21.8 3.9 %shard_map.79 = (f32[8,136,128]{2,1,0:T(8,128)S(1)}, f32[8,136,128]{2,1,0:T(8,128)S(1)}, f32[2,8,136,128]{3,2,1,0:T(8,128)}) custom-call(bf16[1024,2048]{1,0:T(8,128)(2,1)S(1)} %get-tuple-element.21.refs_2_.stack_ref, bf16[1024,256]{1,0:T(8,128)(2,1)S(1)} %get-tuple-element.24.edge_ref, bf16[136,2176]{1,0:T(8,128)(2,1)S(1)} %get-tuple-element.25.resid_ref), custom_call_target="tpu_custom_call" | custom-call | flops 2281701376 | bytes 4194304 | tf_op jit(solution)/shard_map/pallas_call | solution.py:369
  26.1 1.6 %collective-permute-start.8 = (bf16[16,32,128]{2,1,0:T(8,128)(2,1)S(1)}, bf16[16,32,128]{2,1,0:T(8,128)(2,1)S(1)}, u32[]{:S(2)}, u32[]{:S(2)}) collective-permute-start(bf16[16,32,128]{2,1,0:T(8,128)(2,1)S(1)} %get-tuple-element.32), channel_id=1, source_target_pairs={{0,4},{4,8},{8,12},{12,0},{16,20},{20,24},{24,28},{28,16},{32,36},... | collective-permute-start | bytes 393224 | tf_op jit(solution)/shard_map/ppermute | solution.py:30
  27.7 2.9 %collective-permute-start.9 = (bf16[16,32,128]{2,1,0:T(8,128)(2,1)S(1)}, bf16[16,32,128]{2,1,0:T(8,128)(2,1)S(1)}, u32[]{:S(2)}, u32[]{:S(2)}) collective-permute-start(bf16[16,32,128]{2,1,0:T(8,128)(2,1)S(1)} %get-tuple-element.33), channel_id=1, source_target_pairs={{0,8},{4,12},{8,0},{12,4},{16,24},{20,28},{24,16},{28,20},{32,40},... | collective-permute-start | bytes 393224 | tf_op jit(solution)/shard_map/ppermute | solution.py:30
  30.6 1.3 %collective-permute-start.10 = (bf16[16,32,128]{2,1,0:T(8,128)(2,1)S(1)}, bf16[16,32,128]{2,1,0:T(8,128)(2,1)S(1)}, u32[]{:S(2)}, u32[]{:S(2)}) collective-permute-start(bf16[16,32,128]{2,1,0:T(8,128)(2,1)S(1)} %get-tuple-element.34), channel_id=1, source_target_pairs={{0,12},{4,0},{8,4},{12,8},{16,28},{20,16},{24,20},{28,24},{32,44},... | collective-permute-start | bytes 393224 | tf_op jit(solution)/shard_map/ppermute | solution.py:30
  31.9 1.2 %collective-permute-done.8.refs_1_ = bf16[16,32,128]{2,1,0:T(8,128)(2,1)S(1)} collective-permute-done((bf16[16,32,128]{2,1,0:T(8,128)(2,1)S(1)}, bf16[16,32,128]{2,1,0:T(8,128)(2,1)S(1)}, u32[]{:S(2)}, u32[]{:S(2)}) %collective-permute-start.8) | collective-permute-done | bytes 131104 | tf_op jit(solution)/shard_map/ppermute | solution.py:30
  33.2 4.0 %collective-permute-done.9.refs_2_ = bf16[16,32,128]{2,1,0:T(8,128)(2,1)S(1)} collective-permute-done((bf16[16,32,128]{2,1,0:T(8,128)(2,1)S(1)}, bf16[16,32,128]{2,1,0:T(8,128)(2,1)S(1)}, u32[]{:S(2)}, u32[]{:S(2)}) %collective-permute-start.9) | collective-permute-done | bytes 131104 | tf_op jit(solution)/shard_map/ppermute | solution.py:30
  37.2 21.1 %all_to_all.10.parts_ref = bf16[16,32,128]{2,1,0:T(8,128)(2,1)S(1)} all-to-all(bf16[16,32,128]{2,1,0:T(8,128)(2,1)S(1)} %shard_map.82), channel_id=1, replica_groups={{0,16,32,48,64,80,96,112,128,144,160,176,192,208,224,240},{4,20,36,52,6..., dimensions={0} | all-to-all | bytes 262144 | tf_op jit(solution)/shard_map/all_to_all | solution.py:35
  59.0 3.5 %all-to-all-start.1 = ((bf16[16,32,128]{2,1,0:T(8,128)(2,1)}), bf16[16,32,128]{2,1,0:T(8,128)(2,1)S(1)}, u32[]{:S(2)}, u32[]{:S(2)}) async-start(bf16[16,32,128]{2,1,0:T(8,128)(2,1)} %shard_map.83), calls=%async_computation.1 | async-start | bytes 262144 | tf_op jit(solution)/shard_map/all_to_all | solution.py:35
  62.6 1.5 %collective-permute-start.7 = (bf16[10,136,128]{2,1,0:T(8,128)(2,1)S(1)}, bf16[10,136,128]{2,1,0:T(8,128)(2,1)S(1)}, u32[]{:S(2)}, u32[]{:S(2)}) collective-permute-start(bf16[10,136,128]{2,1,0:T(8,128)(2,1)S(1)} %shard_map.80), channel_id=1, source_target_pairs={{0,2},{1,3},{2,0},{3,1},{4,6},{5,7},{6,4},{7,5},{8,10},{9,11},{10,... | collective-permute-start | bytes 1044488 | tf_op jit(solution)/shard_map/ppermute | solution.py:25
  64.1 9.6 %all-to-all-done.1.parts_ref = bf16[16,32,128]{2,1,0:T(8,128)(2,1)S(1)} async-done(((bf16[16,32,128]{2,1,0:T(8,128)(2,1)}), bf16[16,32,128]{2,1,0:T(8,128)(2,1)S(1)}, u32[]{:S(2)}, u32[]{:S(2)}) %all-to-all-start.1) | async-done | bytes 131104 | tf_op jit(solution)/shard_map/all_to_all | solution.py:35
  73.7 2.1 %collective-permute-start.13 = (bf16[32,2048]{1,0:T(8,128)(2,1)S(1)}, bf16[32,2048]{1,0:T(8,128)(2,1)S(1)}, u32[]{:S(2)}, u32[]{:S(2)}) collective-permute-start(bf16[32,2048]{1,0:T(8,128)(2,1)S(1)} %shard_map.84.refs_0_), channel_id=1, source_target_pairs={{0,12},{4,0},{8,4},{12,8},{16,28},{20,16},{24,20},{28,24},{32,44},... | collective-permute-start | bytes 393224 | tf_op jit(solution)/shard_map/ppermute | solution.py:30
  75.9 1.1 %collective-permute-start.12 = (bf16[32,2048]{1,0:T(8,128)(2,1)S(1)}, bf16[32,2048]{1,0:T(8,128)(2,1)S(1)}, u32[]{:S(2)}, u32[]{:S(2)}) collective-permute-start(bf16[32,2048]{1,0:T(8,128)(2,1)S(1)} %shard_map.84.refs_0_), channel_id=1, source_target_pairs={{0,8},{4,12},{8,0},{12,4},{16,24},{20,28},{24,16},{28,20},{32,40},... | collective-permute-start | bytes 393224 | tf_op jit(solution)/shard_map/ppermute | solution.py:30
  77.8 1.0 %collective-permute-done.13.refs_3_ = bf16[32,2048]{1,0:T(8,128)(2,1)S(1)} collective-permute-done((bf16[32,2048]{1,0:T(8,128)(2,1)S(1)}, bf16[32,2048]{1,0:T(8,128)(2,1)S(1)}, u32[]{:S(2)}, u32[]{:S(2)}) %collective-permute-start.13) | collective-permute-done | bytes 131104 | tf_op jit(solution)/shard_map/ppermute | solution.py:30
  78.8 3.6 %collective-permute-done.12.refs_2_ = bf16[32,2048]{1,0:T(8,128)(2,1)S(1)} collective-permute-done((bf16[32,2048]{1,0:T(8,128)(2,1)S(1)}, bf16[32,2048]{1,0:T(8,128)(2,1)S(1)}, u32[]{:S(2)}, u32[]{:S(2)}) %collective-permute-start.12) | collective-permute-done | bytes 131104 | tf_op jit(solution)/shard_map/ppermute | solution.py:30
  82.4 1.3 %collective-permute-done.11.refs_1_ = bf16[32,2048]{1,0:T(8,128)(2,1)S(1)} collective-permute-done((bf16[32,2048]{1,0:T(8,128)(2,1)S(1)}, bf16[32,2048]{1,0:T(8,128)(2,1)S(1)}, u32[]{:S(2)}, u32[]{:S(2)}) %collective-permute-start.11) | collective-permute-done | bytes 131104 | tf_op jit(solution)/shard_map/ppermute | solution.py:30
  83.8 0.8 shard_map.85
  84.6 1.0 %shard_map.81 = (bf16[8,128,128]{2,1,0:T(8,128)(2,1)}, bf16[8,8,128]{2,1,0:T(8,128)(2,1)}) custom-call(bf16[8,128,128]{2,1,0:T(8,128)(2,1)S(1)} %copy-done.2, bf16[8,8,128]{2,1,0:T(8,128)(2,1)S(1)} %copy-done.3, f32[8,136,128]{2,1,0:T(8,128)S(1)} %get-tuple-element.26.keep_ref, f32[2,8,136,128]{3,2,1,0:T(8,128)S(1)} %collective-permute-done.6.got_ref, ...), custom_call_target="tpu_custom_call" | custom-call | bytes 4194304 | tf_op jit(solution)/shard_map/pallas_call | solution.py:369
  (27 shorter events, 3.0 us)
Async XLA Ops:
  0.6 15.7 %copy-start.2 = (bf16[8,128,128]{2,1,0:T(8,128)(2,1)S(1)}, bf16[8,128,128]{2,1,0:T(8,128)(2,1)}, u32[]{:S(2)}) copy-start(bf16[8,128,128]{2,1,0:T(8,128)(2,1)} %w_ref.1) | copy-start | bytes 786436
  0.6 15.7 %copy-start.4 = (bf16[8,2048]{1,0:T(8,128)(2,1)S(1)}, bf16[8,2048]{1,0:T(8,128)(2,1)}, u32[]{:S(2)}) copy-start(bf16[8,2048]{1,0:T(8,128)(2,1)} %refs_5_.1) | copy-start | bytes 98308
  0.7 15.7 %copy-start = (bf16[128,2048]{1,0:T(8,128)(2,1)S(1)}, bf16[128,2048]{1,0:T(8,128)(2,1)}, u32[]{:S(2)}) copy-start(bf16[128,2048]{1,0:T(8,128)(2,1)} %refs_4_.1) | copy-start | bytes 1572868
  0.7 8.3 %collective-permute-start.2 = (bf16[8,128,128]{2,1,0:T(8,128)(2,1)}, bf16[8,128,128]{2,1,0:T(8,128)(2,1)S(1)}, u32[]{:S(2)}, u32[]{:S(2)}) collective-permute-start(bf16[8,128,128]{2,1,0:T(8,128)(2,1)} %w_ref.1), channel_id=1, source_target_pairs={{0,2},{1,3},{2,0},{3,1},{4,6},{5,7},{6,4},{7,5},{8,10},{9,11},{10,... | collective-permute-start | bytes 786440 | tf_op jit(solution)/shard_map/ppermute | solution.py:25
  3.0 9.5 %collective-permute-start = (bf16[8,128,128]{2,1,0:T(8,128)(2,1)}, bf16[8,128,128]{2,1,0:T(8,128)(2,1)S(1)}, u32[]{:S(2)}, u32[]{:S(2)}) collective-permute-start(bf16[8,128,128]{2,1,0:T(8,128)(2,1)} %w_ref.1), channel_id=1, source_target_pairs={{0,1},{1,0},{2,3},{3,2},{4,5},{5,4},{6,7},{7,6},{8,9},{9,8},{10,11... | collective-permute-start | bytes 786440 | tf_op jit(solution)/shard_map/ppermute | solution.py:25
  9.0 7.3 %collective-permute-start.3 = (bf16[8,128,128]{2,1,0:T(8,128)(2,1)S(1)}, bf16[8,128,128]{2,1,0:T(8,128)(2,1)S(1)}, u32[]{:S(2)}, u32[]{:S(2)}) collective-permute-start(bf16[8,128,128]{2,1,0:T(8,128)(2,1)S(1)} %collective-permute-done.2.refs_8_), channel_id=1, source_target_pairs={{0,1},{1,0},{2,3},{3,2},{4,5},{5,4},{6,7},{7,6},{8,9},{9,8},{10,11... | collective-permute-start | bytes 786440 | tf_op jit(solution)/shard_map/ppermute | solution.py:25
  10.2 2.3 %collective-permute-start.1 = (bf16[168,128]{1,0:T(8,128)(2,1)S(1)}, bf16[168,128]{1,0:T(8,128)(2,1)S(1)}, u32[]{:S(2)}, u32[]{:S(2)}) collective-permute-start(bf16[168,128]{1,0:T(8,128)(2,1)S(1)} %get-tuple-element.20.p0_ref.refs_10_), channel_id=1, source_target_pairs={{0,1},{1,0},{2,3},{3,2},{4,5},{5,4},{6,7},{7,6},{8,9},{9,8},{10,11... | collective-permute-start | bytes 129032 | tf_op jit(solution)/shard_map/ppermute | solution.py:25
  10.8 5.5 %collective-permute-start.5 = (bf16[168,128]{1,0:T(8,128)(2,1)S(1)}, bf16[168,128]{1,0:T(8,128)(2,1)S(1)}, u32[]{:S(2)}, u32[]{:S(2)}) collective-permute-start(bf16[168,128]{1,0:T(8,128)(2,1)S(1)} %get-tuple-element.20.p0_ref.refs_10_), channel_id=1, source_target_pairs={{0,3},{1,2},{2,1},{3,0},{4,7},{5,6},{6,5},{7,4},{8,11},{9,10},{10,... | collective-permute-start | bytes 129032 | tf_op jit(solution)/shard_map/ppermute | solution.py:25
  11.0 5.3 %collective-permute-start.4 = (bf16[168,128]{1,0:T(8,128)(2,1)S(1)}, bf16[168,128]{1,0:T(8,128)(2,1)S(1)}, u32[]{:S(2)}, u32[]{:S(2)}) collective-permute-start(bf16[168,128]{1,0:T(8,128)(2,1)S(1)} %get-tuple-element.20.p0_ref.refs_10_), channel_id=1, source_target_pairs={{0,2},{1,3},{2,0},{3,1},{4,6},{5,7},{6,4},{7,5},{8,10},{9,11},{10,... | collective-permute-start | bytes 129032 | tf_op jit(solution)/shard_map/ppermute | solution.py:25
  12.5 1.0 %copy-start.1 = (bf16[8,128,128]{2,1,0:T(8,128)(2,1)S(1)}, bf16[8,128,128]{2,1,0:T(8,128)(2,1)}, u32[]{:S(2)}) copy-start(bf16[8,128,128]{2,1,0:T(8,128)(2,1)} %w_ref.1) | copy-start | bytes 786436
  25.7 58.9 %copy-start.3 = (bf16[8,8,128]{2,1,0:T(8,128)(2,1)S(1)}, bf16[8,8,128]{2,1,0:T(8,128)(2,1)}, u32[]{:S(2)}) copy-start(bf16[8,8,128]{2,1,0:T(8,128)(2,1)} %v_ref.1) | copy-start | bytes 49156
  25.7 36.8 %collective-permute-start.6 = (f32[2,8,136,128]{3,2,1,0:T(8,128)}, f32[2,8,136,128]{3,2,1,0:T(8,128)S(1)}, u32[]{:S(2)}, u32[]{:S(2)}) collective-permute-start(f32[2,8,136,128]{3,2,1,0:T(8,128)} %get-tuple-element.27), channel_id=1, source_target_pairs={{0,1},{1,0},{2,3},{3,2},{4,5},{5,4},{6,7},{7,6},{8,9},{9,8},{10,11... | collective-permute-start | bytes 3342344 | tf_op jit(solution)/shard_map/ppermute | solution.py:25
  26.1 7.1 %collective-permute-start.8 = (bf16[16,32,128]{2,1,0:T(8,128)(2,1)S(1)}, bf16[16,32,128]{2,1,0:T(8,128)(2,1)S(1)}, u32[]{:S(2)}, u32[]{:S(2)}) collective-permute-start(bf16[16,32,128]{2,1,0:T(8,128)(2,1)S(1)} %get-tuple-element.32), channel_id=1, source_target_pairs={{0,4},{4,8},{8,12},{12,0},{16,20},{20,24},{24,28},{28,16},{32,36},... | collective-permute-start | bytes 393224 | tf_op jit(solution)/shard_map/ppermute | solution.py:30
  27.7 9.5 %collective-permute-start.9 = (bf16[16,32,128]{2,1,0:T(8,128)(2,1)S(1)}, bf16[16,32,128]{2,1,0:T(8,128)(2,1)S(1)}, u32[]{:S(2)}, u32[]{:S(2)}) collective-permute-start(bf16[16,32,128]{2,1,0:T(8,128)(2,1)S(1)} %get-tuple-element.33), channel_id=1, source_target_pairs={{0,8},{4,12},{8,0},{12,4},{16,24},{20,28},{24,16},{28,20},{32,40},... | collective-permute-start | bytes 393224 | tf_op jit(solution)/shard_map/ppermute | solution.py:30
  30.6 6.6 %collective-permute-start.10 = (bf16[16,32,128]{2,1,0:T(8,128)(2,1)S(1)}, bf16[16,32,128]{2,1,0:T(8,128)(2,1)S(1)}, u32[]{:S(2)}, u32[]{:S(2)}) collective-permute-start(bf16[16,32,128]{2,1,0:T(8,128)(2,1)S(1)} %get-tuple-element.34), channel_id=1, source_target_pairs={{0,12},{4,0},{8,4},{12,8},{16,28},{20,16},{24,20},{28,24},{32,44},... | collective-permute-start | bytes 393224 | tf_op jit(solution)/shard_map/ppermute | solution.py:30
  59.0 14.7 %all-to-all-start.1 = ((bf16[16,32,128]{2,1,0:T(8,128)(2,1)}), bf16[16,32,128]{2,1,0:T(8,128)(2,1)S(1)}, u32[]{:S(2)}, u32[]{:S(2)}) async-start(bf16[16,32,128]{2,1,0:T(8,128)(2,1)} %shard_map.83), calls=%async_computation.1 | async-start | bytes 262144 | tf_op jit(solution)/shard_map/all_to_all | solution.py:35
  62.6 22.0 %collective-permute-start.7 = (bf16[10,136,128]{2,1,0:T(8,128)(2,1)S(1)}, bf16[10,136,128]{2,1,0:T(8,128)(2,1)S(1)}, u32[]{:S(2)}, u32[]{:S(2)}) collective-permute-start(bf16[10,136,128]{2,1,0:T(8,128)(2,1)S(1)} %shard_map.80), channel_id=1, source_target_pairs={{0,2},{1,3},{2,0},{3,1},{4,6},{5,7},{6,4},{7,5},{8,10},{9,11},{10,... | collective-permute-start | bytes 1044488 | tf_op jit(solution)/shard_map/ppermute | solution.py:25
  73.7 5.0 %collective-permute-start.13 = (bf16[32,2048]{1,0:T(8,128)(2,1)S(1)}, bf16[32,2048]{1,0:T(8,128)(2,1)S(1)}, u32[]{:S(2)}, u32[]{:S(2)}) collective-permute-start(bf16[32,2048]{1,0:T(8,128)(2,1)S(1)} %shard_map.84.refs_0_), channel_id=1, source_target_pairs={{0,12},{4,0},{8,4},{12,8},{16,28},{20,16},{24,20},{28,24},{32,44},... | collective-permute-start | bytes 393224 | tf_op jit(solution)/shard_map/ppermute | solution.py:30
  75.9 6.5 %collective-permute-start.12 = (bf16[32,2048]{1,0:T(8,128)(2,1)S(1)}, bf16[32,2048]{1,0:T(8,128)(2,1)S(1)}, u32[]{:S(2)}, u32[]{:S(2)}) collective-permute-start(bf16[32,2048]{1,0:T(8,128)(2,1)S(1)} %shard_map.84.refs_0_), channel_id=1, source_target_pairs={{0,8},{4,12},{8,0},{12,4},{16,24},{20,28},{24,16},{28,20},{32,40},... | collective-permute-start | bytes 393224 | tf_op jit(solution)/shard_map/ppermute | solution.py:30
  77.0 6.8 %collective-permute-start.11 = (bf16[32,2048]{1,0:T(8,128)(2,1)S(1)}, bf16[32,2048]{1,0:T(8,128)(2,1)S(1)}, u32[]{:S(2)}, u32[]{:S(2)}) collective-permute-start(bf16[32,2048]{1,0:T(8,128)(2,1)S(1)} %shard_map.84.refs_0_), channel_id=1, source_target_pairs={{0,4},{4,8},{8,12},{12,0},{16,20},{20,24},{24,28},{28,16},{32,36},... | collective-permute-start | bytes 393224 | tf_op jit(solution)/shard_map/ppermute | solution.py:30

commit v4 on v3

--- a/solution.py
+++ b/solution.py
@@ -66,7 +66,7 @@
         copy.wait()
 
 
-def pack(v_hbm, active_hbm, data_hbm, behav_hbm, out_ref, active_ref, v_ref, data_ref, behav_ref, sems):
+def pack(v_hbm, active_hbm, data_hbm, behav_hbm, w_hbm, out_ref, active_ref, w_ref, v_ref, data_ref, behav_ref, sems):
     frames = active_hbm.shape[1]
     fetched(
         [
@@ -74,6 +74,7 @@
             (v_hbm, v_ref),
             (data_hbm.at[:, :lane], data_ref),
             (behav_hbm.at[:, :lane], behav_ref),
+            (w_hbm, w_ref),
         ],
         sems,
     )
@@ -356,21 +357,20 @@
 
 
 def join_rows(*refs):
-    parts, out_ref = refs[:wide], refs[wide]
+    parts, out_hbm, sems = refs[:wide], refs[wide], refs[wide + 1]
     _, y = place()
-    for r in range(wide):
-        row = pl.multiple_of((y + wide - r) % wide * patch, patch)
-        out_ref[pl.ds(row, patch), :] = parts[r][...]
-
-
-def call(body, out_shape, scratch, args, flops=0, moves=1 << 20, vmem=8, in_specs=None):
+    targets = [out_hbm.at[pl.ds(pl.multiple_of((y + wide - r) % wide * patch, patch), patch)] for r in range(wide)]
+    fetched(list(zip(parts, targets)), sems)
+
+
+def call(body, out_shape, scratch, args, flops=0, moves=1 << 20, vmem=8, in_specs=None, out_specs=None):
     if in_specs:
         args = [pltpu.with_memory_space_constraint(a, pltpu.HBM) if p is HBM else a for a, p in zip(args, in_specs)]
     return pl.pallas_call(
         body,
         out_shape=out_shape,
         in_specs=in_specs or [VMEM] * len(args),
-        out_specs=jax.tree.map(lambda _: VMEM, out_shape),
+        out_specs=out_specs or jax.tree.map(lambda _: VMEM, out_shape),
         scratch_shapes=scratch,
         compiler_params=pltpu.CompilerParams(vmem_limit_bytes=vmem << 20),
         cost_estimate=pl.CostEstimate(flops=flops, bytes_accessed=moves, transcendentals=0),
@@ -393,17 +393,17 @@
 
     w2 = crossed(motifs, 2)
     w1 = crossed(motifs, 1)
-    p0, active = call(
+    p0, active, w0 = call(
         pack,
-        [shape((pack_rows, width), bf16), shape(activations.shape, bf16)],
+        [shape((pack_rows, width), bf16), shape(activations.shape, bf16), shape(motifs.shape, bf16)],
         [
             pltpu.VMEM(behav_motifs.shape, bf16),
             pltpu.VMEM((neurons, lane), bf16),
             pltpu.VMEM((features, lane), bf16),
-            pltpu.SemaphoreType.DMA((4,)),
+            pltpu.SemaphoreType.DMA((5,)),
         ],
-        [behav_motifs, activations, data, behaviour],
-        in_specs=[HBM] * 4,
+        [behav_motifs, activations, data, behaviour, motifs],
+        in_specs=[HBM] * 5,
     )
     p3 = crossed(p0, 3)
     p2 = crossed(p0, 2)
@@ -417,7 +417,7 @@
             shape((group * width, steps // 2 * neurons), bf16),
         ],
         [],
-        [active, motifs, w1, p0, p1],
+        [active, w0, w1, p0, p1],
         flops=lags * (neurons + features) * width * frames,
         moves=8 << 20,
         vmem=16,
@@ -436,7 +436,7 @@
             pltpu.VMEM((group * width, steps * neurons), bf16),
             pltpu.VMEM((deep * wide, patch, lane), f32),
         ],
-        [half, turned, stack, active, data, behaviour, motifs, w1, w2, w3, p0, p1, p2, p3],
+        [half, turned, stack, active, data, behaviour, w0, w1, w2, w3, p0, p1, p2, p3],
         flops=3 * lags * (neurons + features) * width * frames,
         moves=4 << 20,
         vmem=24,
@@ -482,10 +482,12 @@
         functools.partial(update_motifs, rate_motif * scale),
         [shape(motifs.shape, bf16), shape(behav_motifs.shape, bf16)],
         [],
-        [motifs, behav_motifs, keep, got, far],
+        [w0, behav_motifs, keep, got, far],
         moves=4 << 20,
     )
-    new_active = call(join_rows, shape((width, frames), bf16), [], rows)
+    new_active = call(
+        join_rows, shape((width, frames), bf16), [pltpu.SemaphoreType.DMA((wide,))], rows, out_specs=HBM
+    )
     return (new_motifs, new_behav, new_active)
 
 

time: 85.8 us -> 85.2 us (level)
  local copies, waits for them, and re-layouts: 0.97 us -> 0.01 us
    unnamed x10 -> x6, local copies, waits for them, and re-layouts: 0.97 us -> 0.01 us
  transfers between devices with their start and end apart: 15 -> 15, of which waited for: 7 -> 8; matrix products, arithmetic and copies ran while one was open for 0% -> 0% of each run, Pallas kernels for 7% -> 7%
where the time goes in v4:
time: 85.2 us; the launch traced here: 84.9 us
  waiting for transfers between devices  27 us (32%)
  blocking collectives  21.1 us (25%)
  starting transfers between devices  20 us (23%)
  Pallas kernels  16.1 us (19%)
    all_to_all x1, blocking collectives, exchanged(): lax.all_to_all(blocks, 'neuron', 0, 0, axis_index_groups=groups, tiled=True)  21.1 us
    pallas_call x10, Pallas kernels, call(): pl.pallas_call(body, out_shape=out_shape, in_specs=in_specs or [VMEM] * l...  16.1 us
    ppermute x6, waiting for transfers between devices, around(): return lax.ppermute(shard, 'neuron', pairs)  11.2 us
    ppermute x6, starting transfers between devices, around(): return lax.ppermute(shard, 'neuron', pairs)  9.97 us
    all_to_all x1, waiting for transfers between devices, exchanged(): lax.all_to_all(blocks, 'neuron', 0, 0, axis_index_groups=groups, tiled=True)  9.5 us
    ppermute x8, starting transfers between devices, crossed(): return lax.ppermute(shard, 'tm', [(i, i ^ mask) for i in range(4)])  6.55 us
    ppermute x8, waiting for transfers between devices, crossed(): return lax.ppermute(shard, 'tm', [(i, i ^ mask) for i in range(4)])  6.26 us
    all_to_all x1, starting transfers between devices, exchanged(): lax.all_to_all(blocks, 'neuron', 0, 0, axis_index_groups=groups, tiled=True)  3.51 us
  transfers between devices with their start and end apart: 15, of which 8 were waited for; matrix products, arithmetic and copies ran while one was open for 0% of the time, Pallas kernels for 7%

profile of v4, /device:TPU:2, one launch (start us, length us, event | category | flops | bytes accessed | tf_op | source)
XLA Modules:
  0.0 84.9 jit_solution(2392132828266500660)
XLA Ops:
  0.7 2.3 %collective-permute-start.2 = (bf16[8,128,128]{2,1,0:T(8,128)(2,1)}, bf16[8,128,128]{2,1,0:T(8,128)(2,1)S(1)}, u32[]{:S(2)}, u32[]{:S(2)}) collective-permute-start(bf16[8,128,128]{2,1,0:T(8,128)(2,1)} %w_hbm.1), channel_id=1, source_target_pairs={{0,2},{1,3},{2,0},{3,1},{4,6},{5,7},{6,4},{7,5},{8,10},{9,11},{10,... | collective-permute-start | bytes 786440 | tf_op jit(solution)/shard_map/ppermute | solution.py:25
  3.0 6.0 %collective-permute-done.2.refs_8_ = bf16[8,128,128]{2,1,0:T(8,128)(2,1)S(1)} collective-permute-done((bf16[8,128,128]{2,1,0:T(8,128)(2,1)}, bf16[8,128,128]{2,1,0:T(8,128)(2,1)S(1)}, u32[]{:S(2)}, u32[]{:S(2)}) %collective-permute-start.2) | collective-permute-done | bytes 262176 | tf_op jit(solution)/shard_map/ppermute | solution.py:25
  9.0 1.3 %shard_map.76 = (bf16[168,128]{1,0:T(8,128)(2,1)S(1)}, bf16[128,2048]{1,0:T(8,128)(2,1)S(1)}, bf16[8,128,128]{2,1,0:T(8,128)(2,1)S(1)}) custom-call(bf16[8,8,128]{2,1,0:T(8,128)(2,1)} %v_ref.1, bf16[128,2048]{1,0:T(8,128)(2,1)} %active_hbm.1, bf16[128,2048]{1,0:T(8,128)(2,1)} %refs_4_.1, bf16[8,2048]{1,0:T(8,128)(2,1)} %refs_5_.1, bf16[8,128,128]{2,1,0:T(8,128)(2,1)} %w_hbm.1), custom_call_target="tpu_custom_call" | custom-call | bytes 1048576 | tf_op jit(solution)/shard_map/pallas_call | solution.py:369
  11.2 1.5 %collective-permute-start.4 = (bf16[168,128]{1,0:T(8,128)(2,1)S(1)}, bf16[168,128]{1,0:T(8,128)(2,1)S(1)}, u32[]{:S(2)}, u32[]{:S(2)}) collective-permute-start(bf16[168,128]{1,0:T(8,128)(2,1)S(1)} %get-tuple-element.22.p0_ref.refs_10_), channel_id=1, source_target_pairs={{0,2},{1,3},{2,0},{3,1},{4,6},{5,7},{6,4},{7,5},{8,10},{9,11},{10,... | collective-permute-start | bytes 129032 | tf_op jit(solution)/shard_map/ppermute | solution.py:25
  12.6 2.8 %shard_map.77 = (bf16[1024,2048]{1,0:T(8,128)(2,1)S(1)}, f32[544,2176]{1,0:T(8,128)S(1)}, bf16[512,512]{1,0:T(8,128)(2,1)S(1)}) custom-call(bf16[128,2048]{1,0:T(8,128)(2,1)S(1)} %get-tuple-element.21.active_ref.refs_3_, bf16[8,128,128]{2,1,0:T(8,128)(2,1)S(1)} %get-tuple-element.20.w0_ref.refs_6_.w_ref, ...), custom_call_target="tpu_custom_call" | custom-call | flops 1140850688 | bytes 8388608 | tf_op jit(solution)/shard_map/pallas_call | solution.py:369
  15.7 5.4 %shard_map.78 = (f32[16,32,128]{2,1,0:T(8,128)S(1)}, bf16[16,32,128]{2,1,0:T(8,128)(2,1)S(1)}, bf16[16,32,128]{2,1,0:T(8,128)(2,1)S(1)}, bf16[16,32,128]{2,1,0:T...) custom-call(f32[544,2176]{1,0:T(8,128)S(1)} %get-tuple-element.24.refs_0_, ...), custom_call_target="tpu_custom_call" | custom-call | flops 3422552064 | bytes 4194304 | tf_op jit(solution)/shard_map/pallas_call | solution.py:369
  21.2 3.9 %shard_map.79 = (f32[8,136,128]{2,1,0:T(8,128)S(1)}, f32[8,136,128]{2,1,0:T(8,128)S(1)}, f32[2,8,136,128]{3,2,1,0:T(8,128)}) custom-call(bf16[1024,2048]{1,0:T(8,128)(2,1)S(1)} %get-tuple-element.23.refs_2_.stack_ref, bf16[1024,256]{1,0:T(8,128)(2,1)S(1)} %get-tuple-element.26.edge_ref, bf16[136,2176]{1,0:T(8,128)(2,1)S(1)} %get-tuple-element.27.resid_ref), custom_call_target="tpu_custom_call" | custom-call | flops 2281701376 | bytes 4194304 | tf_op jit(solution)/shard_map/pallas_call | solution.py:369
  25.3 1.7 %collective-permute-start.8 = (bf16[16,32,128]{2,1,0:T(8,128)(2,1)S(1)}, bf16[16,32,128]{2,1,0:T(8,128)(2,1)S(1)}, u32[]{:S(2)}, u32[]{:S(2)}) collective-permute-start(bf16[16,32,128]{2,1,0:T(8,128)(2,1)S(1)} %get-tuple-element.34), channel_id=1, source_target_pairs={{0,4},{4,8},{8,12},{12,0},{16,20},{20,24},{24,28},{28,16},{32,36},... | collective-permute-start | bytes 393224 | tf_op jit(solution)/shard_map/ppermute | solution.py:30
  27.0 2.9 %collective-permute-start.9 = (bf16[16,32,128]{2,1,0:T(8,128)(2,1)S(1)}, bf16[16,32,128]{2,1,0:T(8,128)(2,1)S(1)}, u32[]{:S(2)}, u32[]{:S(2)}) collective-permute-start(bf16[16,32,128]{2,1,0:T(8,128)(2,1)S(1)} %get-tuple-element.35), channel_id=1, source_target_pairs={{0,8},{4,12},{8,0},{12,4},{16,24},{20,28},{24,16},{28,20},{32,40},... | collective-permute-start | bytes 393224 | tf_op jit(solution)/shard_map/ppermute | solution.py:30
  29.9 1.3 %collective-permute-start.10 = (bf16[16,32,128]{2,1,0:T(8,128)(2,1)S(1)}, bf16[16,32,128]{2,1,0:T(8,128)(2,1)S(1)}, u32[]{:S(2)}, u32[]{:S(2)}) collective-permute-start(bf16[16,32,128]{2,1,0:T(8,128)(2,1)S(1)} %get-tuple-element.36), channel_id=1, source_target_pairs={{0,12},{4,0},{8,4},{12,8},{16,28},{20,16},{24,20},{28,24},{32,44},... | collective-permute-start | bytes 393224 | tf_op jit(solution)/shard_map/ppermute | solution.py:30
  31.2 1.3 %collective-permute-done.8.refs_1_ = bf16[16,32,128]{2,1,0:T(8,128)(2,1)S(1)} collective-permute-done((bf16[16,32,128]{2,1,0:T(8,128)(2,1)S(1)}, bf16[16,32,128]{2,1,0:T(8,128)(2,1)S(1)}, u32[]{:S(2)}, u32[]{:S(2)}) %collective-permute-start.8) | collective-permute-done | bytes 131104 | tf_op jit(solution)/shard_map/ppermute | solution.py:30
  32.5 4.0 %collective-permute-done.9.refs_2_ = bf16[16,32,128]{2,1,0:T(8,128)(2,1)S(1)} collective-permute-done((bf16[16,32,128]{2,1,0:T(8,128)(2,1)S(1)}, bf16[16,32,128]{2,1,0:T(8,128)(2,1)S(1)}, u32[]{:S(2)}, u32[]{:S(2)}) %collective-permute-start.9) | collective-permute-done | bytes 131104 | tf_op jit(solution)/shard_map/ppermute | solution.py:30
  36.6 21.1 %all_to_all.10.parts_ref = bf16[16,32,128]{2,1,0:T(8,128)(2,1)S(1)} all-to-all(bf16[16,32,128]{2,1,0:T(8,128)(2,1)S(1)} %shard_map.82), channel_id=1, replica_groups={{0,16,32,48,64,80,96,112,128,144,160,176,192,208,224,240},{4,20,36,52,6..., dimensions={0} | all-to-all | bytes 262144 | tf_op jit(solution)/shard_map/all_to_all | solution.py:35
  58.3 3.5 %all-to-all-start.1 = ((bf16[16,32,128]{2,1,0:T(8,128)(2,1)}), bf16[16,32,128]{2,1,0:T(8,128)(2,1)S(1)}, u32[]{:S(2)}, u32[]{:S(2)}) async-start(bf16[16,32,128]{2,1,0:T(8,128)(2,1)} %shard_map.83), calls=%async_computation.1 | async-start | bytes 262144 | tf_op jit(solution)/shard_map/all_to_all | solution.py:35
  61.9 1.6 %collective-permute-start.7 = (bf16[10,136,128]{2,1,0:T(8,128)(2,1)S(1)}, bf16[10,136,128]{2,1,0:T(8,128)(2,1)S(1)}, u32[]{:S(2)}, u32[]{:S(2)}) collective-permute-start(bf16[10,136,128]{2,1,0:T(8,128)(2,1)S(1)} %shard_map.80), channel_id=1, source_target_pairs={{0,2},{1,3},{2,0},{3,1},{4,6},{5,7},{6,4},{7,5},{8,10},{9,11},{10,... | collective-permute-start | bytes 1044488 | tf_op jit(solution)/shard_map/ppermute | solution.py:25
  63.6 9.5 %all-to-all-done.1.parts_ref = bf16[16,32,128]{2,1,0:T(8,128)(2,1)S(1)} async-done(((bf16[16,32,128]{2,1,0:T(8,128)(2,1)}), bf16[16,32,128]{2,1,0:T(8,128)(2,1)S(1)}, u32[]{:S(2)}, u32[]{:S(2)}) %all-to-all-start.1) | async-done | bytes 131104 | tf_op jit(solution)/shard_map/all_to_all | solution.py:35
  73.1 2.1 %collective-permute-start.13 = (bf16[32,2048]{1,0:T(8,128)(2,1)S(1)}, bf16[32,2048]{1,0:T(8,128)(2,1)S(1)}, u32[]{:S(2)}, u32[]{:S(2)}) collective-permute-start(bf16[32,2048]{1,0:T(8,128)(2,1)S(1)} %shard_map.84.refs_0_), channel_id=1, source_target_pairs={{0,12},{4,0},{8,4},{12,8},{16,28},{20,16},{24,20},{28,24},{32,44},... | collective-permute-start | bytes 393224 | tf_op jit(solution)/shard_map/ppermute | solution.py:30
  75.2 1.1 %collective-permute-start.12 = (bf16[32,2048]{1,0:T(8,128)(2,1)S(1)}, bf16[32,2048]{1,0:T(8,128)(2,1)S(1)}, u32[]{:S(2)}, u32[]{:S(2)}) collective-permute-start(bf16[32,2048]{1,0:T(8,128)(2,1)S(1)} %shard_map.84.refs_0_), channel_id=1, source_target_pairs={{0,8},{4,12},{8,0},{12,4},{16,24},{20,28},{24,16},{28,20},{32,40},... | collective-permute-start | bytes 393224 | tf_op jit(solution)/shard_map/ppermute | solution.py:30
  76.4 0.8 collective-permute-start.11
  77.2 1.0 %collective-permute-done.13.refs_3_ = bf16[32,2048]{1,0:T(8,128)(2,1)S(1)} collective-permute-done((bf16[32,2048]{1,0:T(8,128)(2,1)S(1)}, bf16[32,2048]{1,0:T(8,128)(2,1)S(1)}, u32[]{:S(2)}, u32[]{:S(2)}) %collective-permute-start.13) | collective-permute-done | bytes 131104 | tf_op jit(solution)/shard_map/ppermute | solution.py:30
  78.1 3.6 %collective-permute-done.12.refs_2_ = bf16[32,2048]{1,0:T(8,128)(2,1)S(1)} collective-permute-done((bf16[32,2048]{1,0:T(8,128)(2,1)S(1)}, bf16[32,2048]{1,0:T(8,128)(2,1)S(1)}, u32[]{:S(2)}, u32[]{:S(2)}) %collective-permute-start.12) | collective-permute-done | bytes 131104 | tf_op jit(solution)/shard_map/ppermute | solution.py:30
  81.8 1.3 %collective-permute-done.11.refs_1_ = bf16[32,2048]{1,0:T(8,128)(2,1)S(1)} collective-permute-done((bf16[32,2048]{1,0:T(8,128)(2,1)S(1)}, bf16[32,2048]{1,0:T(8,128)(2,1)S(1)}, u32[]{:S(2)}, u32[]{:S(2)}) %collective-permute-start.11) | collective-permute-done | bytes 131104 | tf_op jit(solution)/shard_map/ppermute | solution.py:30
  83.1 0.8 shard_map.85
  84.0 1.0 %shard_map.81 = (bf16[8,128,128]{2,1,0:T(8,128)(2,1)}, bf16[8,8,128]{2,1,0:T(8,128)(2,1)}) custom-call(bf16[8,128,128]{2,1,0:T(8,128)(2,1)S(1)} %get-tuple-element.20.w0_ref.refs_6_.w_ref, bf16[8,8,128]{2,1,0:T(8,128)(2,1)S(1)} %copy-done.1, f32[8,136,128]{2,1,0:T(8,128)S(1)} %get-tuple-element.28.keep_ref, ...), custom_call_target="tpu_custom_call" | custom-call | bytes 4194304 | tf_op jit(solution)/shard_map/pallas_call | solution.py:369
  (23 shorter events, 2.3 us)
Async XLA Ops:
  0.6 15.1 %copy-start.2 = (bf16[8,2048]{1,0:T(8,128)(2,1)S(1)}, bf16[8,2048]{1,0:T(8,128)(2,1)}, u32[]{:S(2)}) copy-start(bf16[8,2048]{1,0:T(8,128)(2,1)} %refs_5_.1) | copy-start | bytes 98308
  0.6 15.1 %copy-start = (bf16[128,2048]{1,0:T(8,128)(2,1)S(1)}, bf16[128,2048]{1,0:T(8,128)(2,1)}, u32[]{:S(2)}) copy-start(bf16[128,2048]{1,0:T(8,128)(2,1)} %refs_4_.1) | copy-start | bytes 1572868
  0.7 8.3 %collective-permute-start.2 = (bf16[8,128,128]{2,1,0:T(8,128)(2,1)}, bf16[8,128,128]{2,1,0:T(8,128)(2,1)S(1)}, u32[]{:S(2)}, u32[]{:S(2)}) collective-permute-start(bf16[8,128,128]{2,1,0:T(8,128)(2,1)} %w_hbm.1), channel_id=1, source_target_pairs={{0,2},{1,3},{2,0},{3,1},{4,6},{5,7},{6,4},{7,5},{8,10},{9,11},{10,... | collective-permute-start | bytes 786440 | tf_op jit(solution)/shard_map/ppermute | solution.py:25
  3.0 9.6 %collective-permute-start = (bf16[8,128,128]{2,1,0:T(8,128)(2,1)}, bf16[8,128,128]{2,1,0:T(8,128)(2,1)S(1)}, u32[]{:S(2)}, u32[]{:S(2)}) collective-permute-start(bf16[8,128,128]{2,1,0:T(8,128)(2,1)} %w_hbm.1), channel_id=1, source_target_pairs={{0,1},{1,0},{2,3},{3,2},{4,5},{5,4},{6,7},{7,6},{8,9},{9,8},{10,11... | collective-permute-start | bytes 786440 | tf_op jit(solution)/shard_map/ppermute | solution.py:25
  9.0 6.7 %collective-permute-start.3 = (bf16[8,128,128]{2,1,0:T(8,128)(2,1)S(1)}, bf16[8,128,128]{2,1,0:T(8,128)(2,1)S(1)}, u32[]{:S(2)}, u32[]{:S(2)}) collective-permute-start(bf16[8,128,128]{2,1,0:T(8,128)(2,1)S(1)} %collective-permute-done.2.refs_8_), channel_id=1, source_target_pairs={{0,1},{1,0},{2,3},{3,2},{4,5},{5,4},{6,7},{7,6},{8,9},{9,8},{10,11... | collective-permute-start | bytes 786440 | tf_op jit(solution)/shard_map/ppermute | solution.py:25
  10.3 2.3 %collective-permute-start.1 = (bf16[168,128]{1,0:T(8,128)(2,1)S(1)}, bf16[168,128]{1,0:T(8,128)(2,1)S(1)}, u32[]{:S(2)}, u32[]{:S(2)}) collective-permute-start(bf16[168,128]{1,0:T(8,128)(2,1)S(1)} %get-tuple-element.22.p0_ref.refs_10_), channel_id=1, source_target_pairs={{0,1},{1,0},{2,3},{3,2},{4,5},{5,4},{6,7},{7,6},{8,9},{9,8},{10,11... | collective-permute-start | bytes 129032 | tf_op jit(solution)/shard_map/ppermute | solution.py:25
  10.9 4.6 %collective-permute-start.5 = (bf16[168,128]{1,0:T(8,128)(2,1)S(1)}, bf16[168,128]{1,0:T(8,128)(2,1)S(1)}, u32[]{:S(2)}, u32[]{:S(2)}) collective-permute-start(bf16[168,128]{1,0:T(8,128)(2,1)S(1)} %get-tuple-element.22.p0_ref.refs_10_), channel_id=1, source_target_pairs={{0,3},{1,2},{2,1},{3,0},{4,7},{5,6},{6,5},{7,4},{8,11},{9,10},{10,... | collective-permute-start | bytes 129032 | tf_op jit(solution)/shard_map/ppermute | solution.py:25
  11.2 4.6 %collective-permute-start.4 = (bf16[168,128]{1,0:T(8,128)(2,1)S(1)}, bf16[168,128]{1,0:T(8,128)(2,1)S(1)}, u32[]{:S(2)}, u32[]{:S(2)}) collective-permute-start(bf16[168,128]{1,0:T(8,128)(2,1)S(1)} %get-tuple-element.22.p0_ref.refs_10_), channel_id=1, source_target_pairs={{0,2},{1,3},{2,0},{3,1},{4,6},{5,7},{6,4},{7,5},{8,10},{9,11},{10,... | collective-permute-start | bytes 129032 | tf_op jit(solution)/shard_map/ppermute | solution.py:25
  25.0 58.9 %copy-start.1 = (bf16[8,8,128]{2,1,0:T(8,128)(2,1)S(1)}, bf16[8,8,128]{2,1,0:T(8,128)(2,1)}, u32[]{:S(2)}) copy-start(bf16[8,8,128]{2,1,0:T(8,128)(2,1)} %v_ref.1) | copy-start | bytes 49156
  25.1 36.8 %collective-permute-start.6 = (f32[2,8,136,128]{3,2,1,0:T(8,128)}, f32[2,8,136,128]{3,2,1,0:T(8,128)S(1)}, u32[]{:S(2)}, u32[]{:S(2)}) collective-permute-start(f32[2,8,136,128]{3,2,1,0:T(8,128)} %get-tuple-element.29), channel_id=1, source_target_pairs={{0,1},{1,0},{2,3},{3,2},{4,5},{5,4},{6,7},{7,6},{8,9},{9,8},{10,11... | collective-permute-start | bytes 3342344 | tf_op jit(solution)/shard_map/ppermute | solution.py:25
  25.3 7.2 %collective-permute-start.8 = (bf16[16,32,128]{2,1,0:T(8,128)(2,1)S(1)}, bf16[16,32,128]{2,1,0:T(8,128)(2,1)S(1)}, u32[]{:S(2)}, u32[]{:S(2)}) collective-permute-start(bf16[16,32,128]{2,1,0:T(8,128)(2,1)S(1)} %get-tuple-element.34), channel_id=1, source_target_pairs={{0,4},{4,8},{8,12},{12,0},{16,20},{20,24},{24,28},{28,16},{32,36},... | collective-permute-start | bytes 393224 | tf_op jit(solution)/shard_map/ppermute | solution.py:30
  27.0 9.5 %collective-permute-start.9 = (bf16[16,32,128]{2,1,0:T(8,128)(2,1)S(1)}, bf16[16,32,128]{2,1,0:T(8,128)(2,1)S(1)}, u32[]{:S(2)}, u32[]{:S(2)}) collective-permute-start(bf16[16,32,128]{2,1,0:T(8,128)(2,1)S(1)} %get-tuple-element.35), channel_id=1, source_target_pairs={{0,8},{4,12},{8,0},{12,4},{16,24},{20,28},{24,16},{28,20},{32,40},... | collective-permute-start | bytes 393224 | tf_op jit(solution)/shard_map/ppermute | solution.py:30
  29.9 6.6 %collective-permute-start.10 = (bf16[16,32,128]{2,1,0:T(8,128)(2,1)S(1)}, bf16[16,32,128]{2,1,0:T(8,128)(2,1)S(1)}, u32[]{:S(2)}, u32[]{:S(2)}) collective-permute-start(bf16[16,32,128]{2,1,0:T(8,128)(2,1)S(1)} %get-tuple-element.36), channel_id=1, source_target_pairs={{0,12},{4,0},{8,4},{12,8},{16,28},{20,16},{24,20},{28,24},{32,44},... | collective-permute-start | bytes 393224 | tf_op jit(solution)/shard_map/ppermute | solution.py:30
  58.3 14.8 %all-to-all-start.1 = ((bf16[16,32,128]{2,1,0:T(8,128)(2,1)}), bf16[16,32,128]{2,1,0:T(8,128)(2,1)S(1)}, u32[]{:S(2)}, u32[]{:S(2)}) async-start(bf16[16,32,128]{2,1,0:T(8,128)(2,1)} %shard_map.83), calls=%async_computation.1 | async-start | bytes 262144 | tf_op jit(solution)/shard_map/all_to_all | solution.py:35
  61.9 22.0 %collective-permute-start.7 = (bf16[10,136,128]{2,1,0:T(8,128)(2,1)S(1)}, bf16[10,136,128]{2,1,0:T(8,128)(2,1)S(1)}, u32[]{:S(2)}, u32[]{:S(2)}) collective-permute-start(bf16[10,136,128]{2,1,0:T(8,128)(2,1)S(1)} %shard_map.80), channel_id=1, source_target_pairs={{0,2},{1,3},{2,0},{3,1},{4,6},{5,7},{6,4},{7,5},{8,10},{9,11},{10,... | collective-permute-start | bytes 1044488 | tf_op jit(solution)/shard_map/ppermute | solution.py:25
  73.1 5.0 %collective-permute-start.13 = (bf16[32,2048]{1,0:T(8,128)(2,1)S(1)}, bf16[32,2048]{1,0:T(8,128)(2,1)S(1)}, u32[]{:S(2)}, u32[]{:S(2)}) collective-permute-start(bf16[32,2048]{1,0:T(8,128)(2,1)S(1)} %shard_map.84.refs_0_), channel_id=1, source_target_pairs={{0,12},{4,0},{8,4},{12,8},{16,28},{20,16},{24,20},{28,24},{32,44},... | collective-permute-start | bytes 393224 | tf_op jit(solution)/shard_map/ppermute | solution.py:30
  75.2 6.5 %collective-permute-start.12 = (bf16[32,2048]{1,0:T(8,128)(2,1)S(1)}, bf16[32,2048]{1,0:T(8,128)(2,1)S(1)}, u32[]{:S(2)}, u32[]{:S(2)}) collective-permute-start(bf16[32,2048]{1,0:T(8,128)(2,1)S(1)} %shard_map.84.refs_0_), channel_id=1, source_target_pairs={{0,8},{4,12},{8,0},{12,4},{16,24},{20,28},{24,16},{28,20},{32,40},... | collective-permute-start | bytes 393224 | tf_op jit(solution)/shard_map/ppermute | solution.py:30
  76.4 6.7 %collective-permute-start.11 = (bf16[32,2048]{1,0:T(8,128)(2,1)S(1)}, bf16[32,2048]{1,0:T(8,128)(2,1)S(1)}, u32[]{:S(2)}, u32[]{:S(2)}) collective-permute-start(bf16[32,2048]{1,0:T(8,128)(2,1)S(1)} %shard_map.84.refs_0_), channel_id=1, source_target_pairs={{0,4},{4,8},{8,12},{12,0},{16,20},{20,24},{24,28},{28,16},{32,36},... | collective-permute-start | bytes 393224 | tf_op jit(solution)/shard_map/ppermute | solution.py:30
